TPU v7x, 512 devices: a whole 4x8x8 slice. The times are simulated.
512 devices in a mesh: energy: 256 (over z, y, x), slab: 2 (over core).
Axes of the slice: x: 4, y: 8, z: 8, core: 2. Of those that a mesh axis runs over, the one named last changes fastest.
Arguments:
- hamiltonian: float32 [4, 128, 128], P('slab'), may hold values from -2 to 2, as said below
- coupling: float32 [4, 128, 128], P('slab'), may hold values from -0.5 to 0.5
- bonds: int32 [4, 128], P('slab'), may hold values 0 or 1
- phonon_coupling: float32 [4, 128], P('slab'), may hold values from 0.1 to 1
- previous_green: float32 [512, 4, 2, 128], P('energy', 'slab'), may hold values from -2.5 to 2.5, as said below
- phonon_shift: int32 [4], P('slab'), may hold values from 1 to 2
Outputs:
- green_blocks: float32 [512, 4, 2, 128, 128], P('energy', 'slab')
- density: float32 [4, 128], P('slab')
Inputs may be any that keep to these rules, and one draw needn't show every extreme that they name: Every hamiltonian block is symmetric. `previous_green`: the imaginary parts (index 1 of the third dimension) are negative.
All inputs are finite; a program needn't handle non-finite values. No bound on the sum of `bonds` on one device may be relied on, other than what follows from the above.
Results may differ from a plain program's by a relative error of at most 0.0001.
Values sent between devices are 32-bit elements; how exact they have to be, the bound alone decides.
A program may use at most 128 MiB of HBM per device.

v0:
```python
import functools

import jax
import jax.numpy as jnp
from jax import lax
from jax.sharding import Mesh
from jax.sharding import PartitionSpec as P

ENERGY = ("energy_0", "energy_1", "energy_2")


HIGHEST = lax.Precision.HIGHEST
BROADENING = 0.2
LEAD_WIDTH = 0.5
THERMAL = 0.1
HALF_WINDOW = 3.0


def with_halo(x, sides, width):
    for axis, dim in sides:
        size, length = (lax.axis_size(axis), x.shape[dim])
        up = [(i, (i + 1) % size) for i in range(size - 1)]
        down = [(j, i) for i, j in up]
        last = lax.slice_in_dim(x, length - width, length, axis=dim)
        leading = lax.slice_in_dim(x, 0, width, axis=dim)
        before = lax.ppermute(last, axis, up)
        after = lax.ppermute(leading, axis, down)
        x = jnp.concatenate([before, x, after], axis=dim)
    return x


def from_behind(x, axis, by):
    length = lax.axis_size(axis)
    pairs = [(i, i + by) for i in range(length) if 0 <= i + by < length]
    return lax.ppermute(x, axis, pairs)


def over_axes(x, axes):
    return functools.reduce(lax.psum, axes, x)


def product(left, right):
    return jnp.matmul(left, right, precision=HIGHEST)


def chol_apply(factor, right_side):
    inner = lax.linalg.triangular_solve(factor, right_side, left_side=True, lower=True)
    return lax.linalg.triangular_solve(factor, inner, left_side=True, lower=True, transpose_a=True)


def invert(blocks):
    real_part = blocks[:, 0]
    imag_part = blocks[:, 1]
    lower_imag = jnp.linalg.cholesky(imag_part)
    ratio_matrix = chol_apply(lower_imag, real_part)
    schur_block = imag_part + product(real_part, ratio_matrix)
    lower_schur = jnp.linalg.cholesky(schur_block)
    identity = jnp.broadcast_to(
        jnp.eye(schur_block.shape[-1], dtype=schur_block.dtype), schur_block.shape
    )
    imag_inverse = -chol_apply(lower_schur, identity)
    real_inverse = -product(ratio_matrix, imag_inverse)
    return jnp.stack([real_inverse, imag_inverse], axis=1)


def project_left(weight, blocks):
    return product(product(weight.T, blocks), weight)


def project_right(weight, blocks):
    return product(product(weight, blocks), weight.T)


def slab_matrix(hamiltonian_block, phonon_self, energy_grid):
    identity = jnp.eye(hamiltonian_block.shape[0], dtype=jnp.float32)
    real_part = (
        energy_grid[:, None, None] * identity
        - hamiltonian_block
        - phonon_self[:, 0, None, :] * identity
    )
    imag_part = BROADENING * identity - phonon_self[:, 1, None, :] * identity
    return jnp.stack([real_part, imag_part], axis=1)


def sweep_left(matrices, weights, blocks):
    selves = []
    for local_slab in range(matrices.shape[0]):
        self_left = project_left(weights[local_slab], blocks)
        selves.append(self_left)
        blocks = invert(matrices[local_slab] - self_left)
    return (blocks, jnp.stack(selves))


def sweep_right(matrices, weights, blocks):
    selves = []
    for local_slab in reversed(range(matrices.shape[0])):
        selves.append(blocks)
        blocks = project_right(weights[local_slab], invert(matrices[local_slab] - blocks))
    return (blocks, jnp.stack(selves[::-1]))


def build_matrices(hamiltonian, phonon_coupling, shifts, padded, energy_grid, first, count, margin):
    built = []
    for local_slab in range(hamiltonian.shape[0]):
        shift_steps = shifts[local_slab]
        column = padded[:, local_slab]
        below_shift = lax.dynamic_slice_in_dim(column, margin + first - shift_steps, count, 0)
        above_shift = lax.dynamic_slice_in_dim(column, margin + first + shift_steps, count, 0)
        phonon_self = phonon_coupling[local_slab] * (below_shift + above_shift)
        built.append(slab_matrix(hamiltonian[local_slab], phonon_self, energy_grid))
    return jnp.stack(built)


def shards(hamiltonian, coupling, bonds, phonon_coupling, previous_green, phonon_shift):
    energy_count = previous_green.shape[0]
    orbitals = hamiltonian.shape[1]
    slab_count = lax.axis_size("slab")
    slab_rank = lax.axis_index("slab")
    energy_total = energy_count * lax.axis_size(ENERGY)
    first_energy = lax.axis_index(ENERGY) * energy_count
    energy_grid = (
        -HALF_WINDOW
        + 2.0
        * HALF_WINDOW
        * ((jnp.arange(energy_count, dtype=jnp.int32) + first_energy).astype(jnp.float32) + 0.5)
        / energy_total
    )
    padded = with_halo(previous_green, ((ENERGY, 0),), energy_count)
    weights = coupling * bonds[:, None, :].astype(jnp.float32)
    identity = jnp.eye(orbitals, dtype=jnp.float32)
    zeros_block = jnp.zeros_like(identity)
    lead_left = jnp.stack([zeros_block, -identity])
    lead_right = jnp.stack([zeros_block, -LEAD_WIDTH * identity])
    matrices = build_matrices(
        hamiltonian,
        phonon_coupling,
        phonon_shift,
        padded,
        energy_grid,
        0,
        energy_count,
        energy_count,
    )
    left_store = jnp.zeros(matrices.shape, jnp.float32)
    right_store = jnp.zeros(matrices.shape, jnp.float32)
    left_received = jnp.broadcast_to(lead_left, matrices.shape[1:])
    right_received = jnp.broadcast_to(lead_right, matrices.shape[1:])
    left_outbox = jnp.zeros(matrices.shape[1:], jnp.float32)
    right_outbox = jnp.zeros(matrices.shape[1:], jnp.float32)
    for sweep_turn in range(slab_count):
        left_entering = jnp.where(slab_rank == 0, lead_left, left_received)
        right_entering = jnp.where(slab_rank == slab_count - 1, lead_right, right_received)

        def advance_left(operands):
            return sweep_left(matrices, weights, operands[0])

        def advance_right(operands):
            return sweep_right(matrices, weights, operands[0])

        def remain_still(operands):
            return (operands[1], operands[2])

        left_outbox, left_store = lax.cond(
            slab_rank == sweep_turn,
            advance_left,
            remain_still,
            (left_entering, left_outbox, left_store),
        )
        right_outbox, right_store = lax.cond(
            slab_rank == slab_count - 1 - sweep_turn,
            advance_right,
            remain_still,
            (right_entering, right_outbox, right_store),
        )
        if sweep_turn + 1 < slab_count:
            left_received = from_behind(left_outbox, "slab", 1)
            right_received = from_behind(right_outbox, "slab", -1)
    combined = matrices - left_store - right_store
    green_local = invert(combined.reshape((-1, 2, orbitals, orbitals))).reshape(combined.shape)
    occupation = jax.nn.sigmoid(-energy_grid / THERMAL)
    diagonal = jnp.diagonal(green_local[:, :, 1], axis1=-2, axis2=-1)
    local_sum = jnp.sum(occupation[None, :, None] * diagonal, axis=1)
    summed = over_axes(local_sum, ENERGY)
    density = -2.0 * HALF_WINDOW / energy_total / jnp.pi * summed
    return (jnp.swapaxes(green_local, 0, 1), density)


def solution(mesh):
    split = Mesh(
        mesh.devices.reshape(8, 8, 4, mesh.shape["slab"]),
        ("energy_0", "energy_1", "energy_2", "slab"),
    )
    in_specs = (
        P("slab", None, None),
        P("slab", None, None),
        P("slab", None),
        P("slab", None),
        P(ENERGY, "slab", None, None),
        P("slab"),
    )
    out_specs = (P(ENERGY, "slab", None, None, None), P("slab", None))
    return jax.shard_map(
        shards, mesh=split, in_specs=in_specs, out_specs=out_specs, check_vma=False
    )
```

profile of v0, /device:TPU:6, one launch (start us, length us, event | category | flops | bytes accessed | tf_op | source)
XLA Modules:
  0.0 603.7 jit_solution(11856067047322949300)
XLA Ops:
  0.6 3.4 collective-permute-start
  4.0 2.4 collective-permute-start.1
  6.6 1.3 fusion.130
  7.9 0.8 slice_bitcast_fusion.34
  8.6 0.9 slice_bitcast_fusion.32
  9.5 0.7 convert_element_type.73
  10.2 0.9 broadcast_multiply_fusion
  16.6 0.7 constant_dynamic-update-slice_fusion.1
  17.7 0.7 fusion.125
  18.4 181.6 %conditional.4 = (f32[2,2,128,128]{3,2,0,1:T(8,128)S(1)}, f32[2,2,2,128,128]{4,3,2,1,0:T(8,128)S(1)}) conditional(s32[]{:T(128)} %convert_element_type.72, () %tuple.50, (f32[2,128,128]{2,1,0:T(8,128)S(1)}, f32[2,2,128,128]{2,3,1,0:T(8,128)S(1)}, f32[2,2,128,128]{2,3,0,1:T(8,128)S(1)}, f32[2,2,128,128]{2,3,0,1:T(8,128)S(1)}) %tuple.51), branch_computations={%region_0.1_spmd, %region_1.7_spmd} | conditional | flops 1008206848 | bytes 16621600 | solution.py:163
  19.6 23.5 %custom-call.56 = f32[2,128,128]{2,1,0:T(8,128)S(1)} custom-call(f32[2,128,128]{2,1,0:T(8,128)S(1)} %fusion.4), custom_call_target="Cholesky" | custom-call | tf_op jit(solution)/shard_map/cond/branch_1_fun/jit(cholesky)/cholesky | solution.py:54
  43.4 19.7 %custom-call.58 = f32[2,1,128,128]{2,3,1,0:T(8,128)S(1)} custom-call(f32[2,1,128,128]{3,2,1,0:T(8,128)S(1)} %select_bitcast_fusion.3), custom_call_target="InvertDiagBlocksLowerTriangular" | custom-call | tf_op jit(solution)/shard_map/cond/branch_1_fun/triangular_solve/custom-call.3 | solution.py:48
  63.1 0.4 fusion.17
  63.7 0.4 convolution_add_fusion.1
  64.2 23.5 %custom-call.59 = f32[2,128,128]{2,1,0:T(8,128)S(1)} custom-call(f32[2,128,128]{2,1,0:T(8,128)S(1)} %fusion.16), custom_call_target="Cholesky" | custom-call | tf_op jit(solution)/shard_map/cond/branch_1_fun/jit(cholesky)/cholesky | solution.py:57
  88.0 19.9 %custom-call.61 = f32[2,1,128,128]{2,3,1,0:T(8,128)S(1)} custom-call(f32[2,1,128,128]{3,2,1,0:T(8,128)S(1)} %select_bitcast_fusion.2), custom_call_target="InvertDiagBlocksLowerTriangular" | custom-call | tf_op jit(solution)/shard_map/cond/branch_1_fun/triangular_solve/custom-call.3 | solution.py:48
  107.9 0.4 fusion.13
  108.9 0.6 convolution_bitcast_fusion
  109.4 0.6 fusion.21
  110.4 23.5 %custom-call.62 = f32[2,128,128]{2,1,0:T(8,128)S(1)} custom-call(f32[2,128,128]{2,1,0:T(8,128)S(1)} %fusion.3), custom_call_target="Cholesky" | custom-call | tf_op jit(solution)/shard_map/cond/branch_1_fun/jit(cholesky)/cholesky | solution.py:54
  134.1 19.7 %custom-call.64 = f32[2,1,128,128]{2,3,1,0:T(8,128)S(1)} custom-call(f32[2,1,128,128]{3,2,1,0:T(8,128)S(1)} %select_bitcast_fusion.1), custom_call_target="InvertDiagBlocksLowerTriangular" | custom-call | tf_op jit(solution)/shard_map/cond/branch_1_fun/triangular_solve/custom-call.3 | solution.py:48
  153.8 0.4 fusion.9
  155.0 23.9 %custom-call.65 = f32[2,128,128]{2,1,0:T(8,128)S(1)} custom-call(f32[2,128,128]{2,1,0:T(8,128)S(1)} %fusion.8), custom_call_target="Cholesky" | custom-call | tf_op jit(solution)/shard_map/cond/branch_1_fun/jit(cholesky)/cholesky | solution.py:57
  179.1 19.7 %custom-call.67 = f32[2,1,128,128]{2,3,1,0:T(8,128)S(1)} custom-call(f32[2,1,128,128]{3,2,1,0:T(8,128)S(1)} %select_bitcast_fusion), custom_call_target="InvertDiagBlocksLowerTriangular" | custom-call | tf_op jit(solution)/shard_map/cond/branch_1_fun/triangular_solve/custom-call.3 | solution.py:48
  198.8 0.4 fusion.5
  200.0 0.8 copy.301
  200.8 2.0 collective-permute-start.2
  202.9 14.0 %conditional.6 = (f32[2,2,128,128]{3,2,1,0:T(8,128)S(1)}, f32[2,2,2,128,128]{3,4,1,2,0:T(8,128)S(1)}) conditional(s32[]{:T(128)} %convert_element_type.71, () %tuple.53, (f32[2,2,128,128]{2,3,0,1:T(8,128)S(1)}, f32[2,2,128,128]{2,3,0,1:T(8,128)S(1)}, f32[2,128,128]{2,1,0:T(8,128)S(1)}, f32[2,2,128,128]{2,3,0,1:T(8,128)S(1)}) %tuple.54), branch_computations={%region_6.10_spmd, %region_7.11_spmd} | conditional | flops 1008206848 | bytes 16883744 | solution.py:169
  216.9 0.8 copy.303
  217.7 1.3 collective-permute-start.3
  219.0 0.7 copy.313
  219.8 0.6 iota_compare_fusion.9
  220.4 0.6 iota_compare_fusion.8
  221.0 8.2 %conditional.5 = (f32[2,2,2,128,128]{3,4,1,2,0:T(8,128)S(1)}) conditional(s32[]{:T(128)} %convert_element_type.71, f32[2,2,2,128,128]{4,3,2,1,0:T(8,128)S(1)} %get-tuple-element.80, (pred[]{:T(512)}, f32[2,2,128,128]{2,3,1,0:T(8,128)S(1)}, f32[2,2,128,128]{2,3,1,0:T(8,128)}, f32[2,128,128]{2,1,0:T(8,128)S(1)}, f32[2,2,128,128]{2,3,0,1:T(8,128)S(1)}) %tuple.52), branch_computations={%region_4.8_spmd, %region_5.9_spmd} | conditional | flops 705593856 | bytes 10981393 | solution.py:163
  229.2 91.7 %conditional.7 = (f32[2,2,2,128,128]{3,4,1,2,0:T(8,128)S(1)}) conditional(s32[]{:T(128)} %convert_element_type.72, f32[2,2,2,128,128]{3,4,1,2,0:T(8,128)S(1)} %get-tuple-element.82, (pred[]{:T(512)}, f32[2,2,128,128]{2,3,0,1:T(8,128)S(1)}, f32[2,2,128,128]{2,3,0,1:T(8,128)}, f32[2,2,128,128]{2,3,0,1:T(8,128)S(1)}, ...), branch_computations={%region_8.12_spmd, %region_9.13_spmd} | conditional | flops 504267264 | bytes 8491025 | solution.py:169
  229.2 1.0 fusion.102
  230.4 23.5 %custom-call.86 = f32[2,128,128]{2,1,0:T(8,128)S(1)} custom-call(f32[2,128,128]{2,1,0:T(8,128)S(1)} %fusion.92), custom_call_target="Cholesky" | custom-call | tf_op jit(solution)/shard_map/cond/branch_1_fun/jit(cholesky)/cholesky | solution.py:54
  254.1 19.7 %custom-call.88 = f32[2,1,128,128]{2,3,1,0:T(8,128)S(1)} custom-call(f32[2,1,128,128]{3,2,1,0:T(8,128)S(1)} %select_bitcast_fusion.11), custom_call_target="InvertDiagBlocksLowerTriangular" | custom-call | tf_op jit(solution)/shard_map/cond/branch_1_fun/triangular_solve/custom-call.3 | solution.py:48
  273.8 0.4 fusion.97
  274.5 0.4 convolution_add_fusion.5
  275.0 23.5 %custom-call.89 = f32[2,128,128]{2,1,0:T(8,128)S(1)} custom-call(f32[2,128,128]{2,1,0:T(8,128)S(1)} %fusion.96), custom_call_target="Cholesky" | custom-call | tf_op jit(solution)/shard_map/cond/branch_1_fun/jit(cholesky)/cholesky | solution.py:57
  298.7 19.9 %custom-call.91 = f32[2,1,128,128]{2,3,1,0:T(8,128)S(1)} custom-call(f32[2,1,128,128]{3,2,1,0:T(8,128)S(1)} %select_bitcast_fusion.10), custom_call_target="InvertDiagBlocksLowerTriangular" | custom-call | tf_op jit(solution)/shard_map/cond/branch_1_fun/triangular_solve/custom-call.3 | solution.py:48
  319.6 0.6 convolution_bitcast_fusion.8
  320.2 0.4 convolution_bitcast_fusion.7
  320.9 1.1 fusion.109
  322.2 46.9 %custom-call.92 = f32[4,128,128]{2,1,0:T(8,128)S(1)} custom-call(f32[4,128,128]{2,1,0:T(8,128)S(1)} %fusion.110), custom_call_target="Cholesky" | custom-call | tf_op jit(solution)/shard_map/jit(cholesky)/cholesky | solution.py:54
  369.1 0.8 select_reduce_fusion.13
  370.0 0.8 select_bitcast_fusion.13
  370.8 39.3 %custom-call.94 = f32[4,1,128,128]{2,3,1,0:T(8,128)S(1)} custom-call(f32[4,1,128,128]{3,2,1,0:T(8,128)S(1)} %select_bitcast_fusion.13), custom_call_target="InvertDiagBlocksLowerTriangular" | custom-call | tf_op jit(solution)/shard_map/triangular_solve/custom-call.5 | solution.py:48
  410.2 0.6 fusion.115
  410.8 0.4 fusion.117
  411.2 0.6 convolution_add_fusion.6
  411.9 46.9 %custom-call.95 = f32[4,128,128]{2,1,0:T(8,128)S(1)} custom-call(f32[4,128,128]{2,1,0:T(8,128)S(1)} %fusion.114), custom_call_target="Cholesky" | custom-call | tf_op jit(solution)/shard_map/jit(cholesky)/cholesky | solution.py:57
  459.1 39.8 %custom-call.97 = f32[4,1,128,128]{2,3,1,0:T(8,128)S(1)} custom-call(f32[4,1,128,128]{3,2,1,0:T(8,128)S(1)} %select_bitcast_fusion.12), custom_call_target="InvertDiagBlocksLowerTriangular" | custom-call | tf_op jit(solution)/shard_map/triangular_solve/custom-call.5 | solution.py:48
  499.0 0.6 fusion.111
  499.6 0.4 convolution_negate_fusion.13
  500.0 0.4 convolution_negate_fusion.12
  500.4 11.4 %copy.317 = f32[2,2,128,128]{1,0,3,2:T(2,128)} copy(f32[2,2,128,128]{3,2,1,0:T(8,128)S(1)} %bitcast.463) | data formatting | bytes 524288 | tf_op jit(solution)/shard_map/squeeze | solution.py:181
  511.8 6.7 %gather_fusion = f32[128,2,2]{2,1,0:T(2,128)S(1)} fusion(f32[2,2,128,128]{1,0,3,2:T(2,128)} %copy.317, s32[128]{0:T(128)S(1)} %or_bitcast_fusion), kind=kCustom, calls=%fused_computation | custom fusion | bytes 5120 | tf_op jit(solution)/shard_map/jit(diagonal)/gather | solution.py:181
  518.7 36.4 %psum.21 = f32[2,128]{0,1:T(8,128)S(1)} all-reduce(f32[2,128]{0,1:T(8,128)S(1)} %bitcast.477), channel_id=1, replica_groups=mesh['energy_0'=8,'energy_1'=8,'energy_2'=4,'slab'=2] {'energy_0'}, use_global_device_ids=true, to_apply=%region_13.20 | all-reduce | flops 256 | bytes 2048 | tf_op jit(solution)/shard_map/psum | solution.py:39
  555.1 31.0 %psum.22 = f32[2,128]{0,1:T(8,128)S(1)} all-reduce(f32[2,128]{0,1:T(8,128)S(1)} %psum.21), channel_id=1, replica_groups=mesh['energy_0'=8,'energy_1'=8,'energy_2'=4,'slab'=2] {'energy_1'}, use_global_device_ids=true, to_apply=%region_14.21 | all-reduce | flops 256 | bytes 2048 | tf_op jit(solution)/shard_map/psum | solution.py:39
  586.0 16.0 %psum.23 = f32[2,128]{0,1:T(8,128)S(1)} all-reduce(f32[2,128]{0,1:T(8,128)S(1)} %psum.22), channel_id=1, replica_groups=mesh['energy_0'=8,'energy_1'=8,'energy_2'=4,'slab'=2] {'energy_2'}, use_global_device_ids=true, to_apply=%region_15.22 | all-reduce | flops 256 | bytes 2048 | tf_op jit(solution)/shard_map/psum | solution.py:39
  602.1 0.6 copy.318
  602.7 0.8 copy_bitcast_fusion
  (105 shorter events, 8.5 us)
Async XLA Ops:
  0.6 16.0 %collective-permute-start = (f32[2,2,2,128]{3,2,1,0:T(2,128)}, f32[2,2,2,128]{3,2,1,0:T(2,128)S(1)}, u32[]{:S(2)}, u32[]{:S(2)}) collective-permute-start(f32[2,2,2,128]{3,2,1,0:T(2,128)} %param.28), channel_id=1, source_target_pairs={{0,2},{2,4},{4,6},{6,8},{8,10},{10,12},{12,14},{14,16},{16,18},{18... | collective-permute-start | bytes 12296 | tf_op jit(solution)/shard_map/ppermute | solution.py:26
  4.0 13.3 %collective-permute-start.1 = (f32[2,2,2,128]{3,2,1,0:T(2,128)}, f32[2,2,2,128]{3,2,1,0:T(2,128)S(1)}, u32[]{:S(2)}, u32[]{:S(2)}) collective-permute-start(f32[2,2,2,128]{3,2,1,0:T(2,128)} %param.28), channel_id=1, source_target_pairs={{2,0},{4,2},{6,4},{8,6},{10,8},{12,10},{14,12},{16,14},{18,16},{20... | collective-permute-start | bytes 12296 | tf_op jit(solution)/shard_map/ppermute | solution.py:27
  200.8 20.1 %collective-permute-start.2 = (f32[2,2,128,128]{2,3,1,0:T(8,128)}, f32[2,2,128,128]{2,3,1,0:T(8,128)}, u32[]{:S(2)}, u32[]{:S(2)}) collective-permute-start(f32[2,2,128,128]{2,3,1,0:T(8,128)} %copy.301), channel_id=1, source_target_pairs={{0,1},{2,3},{4,5},{6,7},{8,9},{10,11},{12,13},{14,15},{16,17},{18,... | collective-permute-start | bytes 786440 | tf_op jit(solution)/shard_map/ppermute | solution.py:35
  217.7 11.4 %collective-permute-start.3 = (f32[2,2,128,128]{2,3,0,1:T(8,128)}, f32[2,2,128,128]{2,3,0,1:T(8,128)}, u32[]{:S(2)}, u32[]{:S(2)}) collective-permute-start(f32[2,2,128,128]{2,3,0,1:T(8,128)} %copy.303), channel_id=1, source_target_pairs={{1,0},{3,2},{5,4},{7,6},{9,8},{11,10},{13,12},{15,14},{17,16},{19,... | collective-permute-start | bytes 786440 | tf_op jit(solution)/shard_map/ppermute | solution.py:35
  229.2 229.7 %copy-start.2 = (pred[128,128]{1,0:T(8,128)(4,1)S(1)}, pred[128,128]{1,0:T(8,128)(4,1)}, u32[]{:S(2)}) copy-start(pred[128,128]{1,0:T(8,128)(4,1)} %iota_compare_fusion.9) | copy-start | bytes 49156
  229.2 229.8 %copy-start.1 = (pred[128,128]{1,0:T(8,128)(4,1)S(1)}, pred[128,128]{1,0:T(8,128)(4,1)}, u32[]{:S(2)}) copy-start(pred[128,128]{1,0:T(8,128)(4,1)} %iota_compare_fusion.8) | copy-start | bytes 49156
  229.2 269.8 %copy-start = (f32[128,128]{1,0:T(8,128)S(1)}, f32[128,128]{1,0:T(8,128)}, u32[]{:S(2)}) copy-start(f32[128,128]{1,0:T(8,128)} %copy.313) | copy-start | bytes 196612
where the time goes:
time: 613 us; the launch traced here: 604 us
  other arithmetic  444 us (72%)
  blocking collectives  83.3 us (14%)
  local copies, waits for them, and re-layouts  26.6 us (4%)
  loops' own time  22.9 us (4%)
  matrix products  11.7 us (2%)
  starting transfers between devices  9.12 us (1%)
  between operations  6.42 us (1%)
    another operation x19, other arithmetic, chol_apply(): lax.linalg.triangular_solve(factor, inner, left_side=True, lower=True, tr...  200 us
    another operation x15, other arithmetic, invert(): lower_imag = jnp.linalg.cholesky(imag_part)  119 us
    another operation x12, other arithmetic, invert(): lower_schur = jnp.linalg.cholesky(schur_block)  118 us
    psum x3, blocking collectives, over_axes(): return functools.reduce(lax.psum, axes, x)  83.3 us
    another operation x2, loops' own time, shards(): lax.cond(slab_rank == slab_count - 1 - sweep_turn, advance_right, remain_...  14.4 us
  transfers between devices with their start and end apart: 4, of which 0 were waited for; matrix products, arithmetic and copies ran while one was open for 1% of the time, Pallas kernels for 0%

commit v1 on v0

v1 whole, which is shorter than its diff:
```python
import functools

import jax
import jax.numpy as jnp
from jax import lax
from jax.experimental import pallas as pl
from jax.experimental.pallas import tpu as pltpu
from jax.sharding import Mesh
from jax.sharding import PartitionSpec as P

ENERGY = ("energy_0", "energy_1", "energy_2")
BROADENING = 0.2
LEAD_WIDTH = 0.5
THERMAL = 0.1
HALF_WINDOW = 3.0
GROUP = 8
PANEL = 32
ROWS = (((0,), (0,)), ((), ()))
PLAIN = (((1,), (0,)), ((), ()))
COLUMNS = (((1,), (1,)), ((), ()))
VMEM = pl.BlockSpec(memory_space=pltpu.VMEM)
SMEM = pl.BlockSpec(memory_space=pltpu.SMEM)


def split(x):
    high = x.astype(jnp.bfloat16)
    return high, (x - high.astype(jnp.float32)).astype(jnp.bfloat16)


def dot(left, right, dims=PLAIN):
    return lax.dot_general(left, right, dims, preferred_element_type=jnp.float32)


def product(left, right, dims=PLAIN):
    (lh, ll), (rh, rl) = split(left), split(right)
    return dot(lh, rh, dims) + (dot(ll, rh, dims) + dot(lh, rl, dims))


def eye(n):
    return lax.broadcasted_iota(jnp.int32, (n, n), 0) == lax.broadcasted_iota(jnp.int32, (n, n), 1)


def eliminate(rows, first):
    count, width = len(rows), rows[0][0].shape[1]
    lane = lax.broadcasted_iota(jnp.int32, (GROUP, width), 1)
    row = lax.broadcasted_iota(jnp.int32, (GROUP, width), 0)

    def column(x, j):
        return jnp.broadcast_to(jnp.sum(jnp.where(lane == j, x, 0.0), axis=1, keepdims=True), x.shape)

    def spread(x, k):
        return jnp.broadcast_to(x[k : k + 1, :], x.shape)

    for g in range(count):
        start = first + g * GROUP
        order = [(g + t) % count for t in range(count)]
        columns = {h: [(column(rows[h][0], start + k), column(rows[h][1], start + k)) for k in range(GROUP)] for h in order}
        pivots = list(columns[g])
        inside = (lane >= start) & (lane < start + GROUP)
        xr = jnp.where(inside, jnp.where(lane == start + row, 1.0, 0.0), rows[g][0])
        xi = jnp.where(inside, 0.0, rows[g][1])
        for k in range(GROUP):
            cr, ci = pivots[k]
            pr, pi = spread(cr, k), spread(ci, k)
            d = 1.0 / (pr * pr + pi * pi)
            qr, qi = pr * d, -(pi * d)
            wr = jnp.where(row == k, 1.0 - qr, cr * qr - ci * qi)
            wi = jnp.where(row == k, -qi, cr * qi + ci * qr)
            for j in range(k + 1, GROUP):
                sr, si = spread(pivots[j][0], k), spread(pivots[j][1], k)
                pivots[j] = (pivots[j][0] - (wr * sr - wi * si), pivots[j][1] - (wr * si + wi * sr))
            sr, si = spread(xr, k), spread(xi, k)
            xr, xi = xr - (wr * sr - wi * si), xi - (wr * si + wi * sr)
        rows[g] = (xr, xi)
        for h in order[1:]:
            yr, yi = jnp.where(inside, 0.0, rows[h][0]), jnp.where(inside, 0.0, rows[h][1])
            for k in range(GROUP):
                cr, ci = columns[h][k]
                sr, si = spread(xr, k), spread(xi, k)
                yr, yi = yr - (cr * sr - ci * si), yi - (cr * si + ci * sr)
            rows[h] = (yr, yi)
    return rows


def invert(real, imag):
    energies, n = real.shape[0], real.shape[-1]
    lane = lax.broadcasted_iota(jnp.int32, (PANEL, n), 1)
    for first in range(0, n, PANEL):
        inside = (lane >= first) & (lane < first + PANEL)
        for e in range(energies):
            before = jnp.concatenate([real[e, first : first + PANEL, :], imag[e, first : first + PANEL, :]], axis=0)
            rows = []
            for at in range(first, first + PANEL, GROUP):
                rows.append((real[e, at : at + GROUP, :], imag[e, at : at + GROUP, :]))
            rows = eliminate(rows, first)
            tr = jnp.concatenate([x for x, _ in rows], axis=0)
            ti = jnp.concatenate([y for _, y in rows], axis=0)
            tr, ti = jnp.where(inside, -tr, tr), jnp.where(inside, -ti, ti)
            after = jnp.concatenate(
                [jnp.concatenate([tr, ti], axis=1), jnp.concatenate([-ti, tr], axis=1)], axis=0
            )
            (lh, ll), (rh, rl) = split(before), split(after)
            update = dot(
                jnp.concatenate([lh, ll, lh, ll], axis=0), jnp.concatenate([rh, rh, rl, rl], axis=0), ROWS
            )
            for at in range(0, n, PANEL):
                s = slice(at, at + PANEL)
                if at == first:
                    real[e, s, :], imag[e, s, :] = tr, ti
                else:
                    real[e, s, :] = jnp.where(inside, 0.0, real[e, s, :]) - update[s, :n]
                    imag[e, s, :] = jnp.where(inside, 0.0, imag[e, s, :]) - update[s, n:]


def pair(real, imag):
    return jnp.concatenate(
        [jnp.concatenate([real, imag], axis=1), jnp.concatenate([-imag, real], axis=1)], axis=0
    )


def chain(role, shifts, grid, ham, weights, strength, own, before, after, outer_x, outer_t, inner_s, inner_x, real, imag):
    energies, n = own.shape[0], ham.shape[-1]
    rank = role[0]
    diagonal = eye(n)

    def build(slab):
        one = shifts[slab] == 1
        around = [before.at[e] for e in range(energies)] + [own.at[e] for e in range(energies)]
        around += [after.at[e] for e in range(energies)]
        blocks = []
        for e in range(energies):
            at = [around[energies + e + step][slab] for step in (-2, -1, 1, 2)]
            green = jnp.where(one, at[1] + at[2], at[0] + at[3])
            self_energy = strength[pl.ds(slab, 1), :] * green
            re = jnp.where(diagonal, grid[e] - self_energy[0:1, :], 0.0) - ham[slab]
            im = jnp.where(diagonal, BROADENING - self_energy[1:2, :], 0.0)
            blocks.append((re, im))
        return blocks

    w_near = weights[0]
    v = weights[1]
    v = jnp.where(rank == 0, v, v.T)
    lead = jnp.where(rank == 0, product(w_near, w_near, ROWS), jnp.where(diagonal, LEAD_WIDTH, 0.0))
    for e, (re, im) in enumerate(build(rank)):
        real[e] = re
        imag[e] = im + lead
    invert(real, imag)
    inner = build(1 - rank)
    for e in range(energies):
        xr, xi = -real[e], -imag[e]
        outer_x[e, 0] = xr
        outer_x[e, 1] = xi
        t = product(jnp.concatenate([xr, xi], axis=0), v)
        tr, ti = t[:n], t[n:]
        outer_t[e, 0] = tr
        outer_t[e, 1] = ti
        self_energy = product(v, jnp.concatenate([tr, ti], axis=1), ROWS)
        re = inner[e][0] - self_energy[:, :n]
        im = inner[e][1] - self_energy[:, n:]
        inner_s[e, 0] = re
        inner_s[e, 1] = im
        real[e] = re
        imag[e] = im
    invert(real, imag)
    for e in range(energies):
        inner_x[e, 0] = -real[e]
        inner_x[e, 1] = -imag[e]


def close(role, occupation, outer_x, outer_t, inner_s, received, w, green, density, real, imag):
    energies, n = outer_x.shape[0], w.shape[-1]
    rank = role[0]
    diagonal = eye(n)
    u = w[...]
    u = jnp.where(rank == 0, u.T, u)
    for e in range(energies):
        t = product(jnp.concatenate([received[e, 0], received[e, 1]], axis=0), u)
        self_energy = product(u, jnp.concatenate([t[:n], t[n:]], axis=1), ROWS)
        real[e] = inner_s[e, 0] - self_energy[:, :n]
        imag[e] = inner_s[e, 1] - self_energy[:, n:]
    invert(real, imag)
    inner_sum = jnp.zeros((1, n), jnp.float32)
    outer_sum = jnp.zeros((1, n), jnp.float32)
    for e in range(energies):
        gr, gi = -real[e], -imag[e]
        green[e, 1 - rank, 0] = gr
        green[e, 1 - rank, 1] = gi
        tr, ti = outer_t[e, 0], outer_t[e, 1]
        y = product(jnp.concatenate([tr, ti], axis=1), pair(gr, gi))
        z = product(y, jnp.concatenate([jnp.concatenate([tr, -ti], axis=1), jnp.concatenate([ti, tr], axis=1)], axis=0), COLUMNS)
        or_, oi = outer_x[e, 0] + z[:, :n], outer_x[e, 1] + z[:, n:]
        green[e, rank, 0] = or_
        green[e, rank, 1] = oi
        inner_sum += occupation[e] * jnp.sum(jnp.where(diagonal, gi, 0.0), axis=0, keepdims=True)
        outer_sum += occupation[e] * jnp.sum(jnp.where(diagonal, oi, 0.0), axis=0, keepdims=True)
    density[pl.ds(rank, 1), :] = outer_sum
    density[pl.ds(1 - rank, 1), :] = inner_sum


def exchange(x):
    return lax.ppermute(x, "slab", [(0, 1), (1, 0)])


def shards(hamiltonian, coupling, bonds, phonon_coupling, previous_green, phonon_shift):
    energies, n = previous_green.shape[0], hamiltonian.shape[1]
    rank = lax.axis_index("slab")
    size = lax.axis_size(ENERGY)
    total = energies * size
    first = lax.axis_index(ENERGY) * energies
    points = (jnp.arange(energies, dtype=jnp.int32) + first).astype(jnp.float32) + 0.5
    grid = -HALF_WINDOW + 2.0 * HALF_WINDOW * points / total
    up = [(i, i + 1) for i in range(size - 1)]
    before = lax.ppermute(previous_green, ENERGY, up)
    after = lax.ppermute(previous_green, ENERGY, [(j, i) for i, j in up])
    weights = coupling * bonds[:, None, :].astype(jnp.float32)
    theirs = exchange(weights[0])
    middle = jnp.where(rank == 0, theirs, weights[0])
    role = jnp.reshape(rank, (1,)).astype(jnp.int32)
    block = jax.ShapeDtypeStruct((energies, 2, n, n), jnp.float32)
    scratch = [pltpu.VMEM((energies, n, n), jnp.float32)] * 2
    outer_x, outer_t, inner_s, inner_x = pl.pallas_call(
        chain,
        out_shape=[block] * 4,
        in_specs=[SMEM] * 3 + [VMEM] * 6,
        out_specs=[VMEM] * 4,
        scratch_shapes=scratch,
        name="chain",
    )(role, phonon_shift, grid, hamiltonian, weights, phonon_coupling, previous_green, before, after)
    received = exchange(inner_x)
    green, partial = pl.pallas_call(
        close,
        out_shape=[
            jax.ShapeDtypeStruct((energies, 2, 2, n, n), jnp.float32),
            jax.ShapeDtypeStruct((2, n), jnp.float32),
        ],
        in_specs=[SMEM] * 2 + [VMEM] * 5,
        out_specs=[VMEM] * 2,
        scratch_shapes=scratch,
        name="close",
    )(role, jax.nn.sigmoid(-grid / THERMAL), outer_x, outer_t, inner_s, received, middle)
    summed = functools.reduce(lax.psum, ENERGY, partial)
    return green, -2.0 * HALF_WINDOW / total / jnp.pi * summed


def solution(mesh):
    split_mesh = Mesh(mesh.devices.reshape(8, 8, 4, mesh.shape["slab"]), (*ENERGY, "slab"))
    in_specs = (
        P("slab", None, None),
        P("slab", None, None),
        P("slab", None),
        P("slab", None),
        P(ENERGY, "slab", None, None),
        P("slab"),
    )
    out_specs = (P(ENERGY, "slab", None, None, None), P("slab", None))
    return jax.shard_map(shards, mesh=split_mesh, in_specs=in_specs, out_specs=out_specs, check_vma=False)
```

time: 613 us -> 93.3 us (0.15)
  the two profiles are of different devices: /device:TPU:6 before, /device:TPU:32 now
where the time goes in v1:
time: 93.3 us; the launch traced here: 92.9 us
  blocking collectives  48.1 us (52%)
  Pallas kernels  23.7 us (25%)
  starting transfers between devices  13.7 us (15%)
  other arithmetic  4.75 us (5%)
  local copies, waits for them, and re-layouts  1.96 us (2%)
    psum x3, blocking collectives, shards(): summed = functools.reduce(lax.psum, ENERGY, partial)  48.1 us
    pallas_call x1, Pallas kernels, shards(): pl.pallas_call(chain, out_shape=[block] * 4, in_specs=[SMEM] * 3 + [VMEM]...  14.1 us
    pallas_call x1, Pallas kernels, shards(): pl.pallas_call(close, out_shape=[jax.ShapeDtypeStruct((energies, 2, 2, n,...  9.61 us
    ppermute x1, starting transfers between devices, shards(): after = lax.ppermute(previous_green, ENERGY, [(j, i) for i, j in up])  5.77 us
    ppermute x2, starting transfers between devices, exchange(): return lax.ppermute(x, 'slab', [(0, 1), (1, 0)])  4.49 us
    ppermute x1, starting transfers between devices, shards(): before = lax.ppermute(previous_green, ENERGY, up)  3.4 us
    unnamed x10, local copies, waits for them, and re-layouts  1.96 us
  transfers between devices with their start and end apart: 4, of which 0 were waited for; matrix products, arithmetic and copies ran while one was open for 5% of the time, Pallas kernels for 15%

profile of v1, /device:TPU:32, one launch (start us, length us, event | category | flops | bytes accessed | tf_op | source)
XLA Modules:
  0.0 92.9 jit_solution(5234785514239487071)
XLA Ops:
  0.6 3.4 %collective-permute-start = (f32[2,2,2,128]{3,2,1,0:T(2,128)}, f32[2,2,2,128]{3,2,1,0:T(2,128)S(1)}, u32[]{:S(2)}, u32[]{:S(2)}) collective-permute-start(f32[2,2,2,128]{3,2,1,0:T(2,128)} %own.1), channel_id=1, source_target_pairs={{0,2},{2,4},{4,6},{6,8},{8,10},{10,12},{12,14},{14,16},{16,18},{18... | collective-permute-start | bytes 12296 | tf_op jit(solution)/shard_map/ppermute | solution.py:213
  4.0 5.8 %collective-permute-start.1 = (f32[2,2,2,128]{3,2,1,0:T(2,128)}, f32[2,2,2,128]{3,2,1,0:T(2,128)S(1)}, u32[]{:S(2)}, u32[]{:S(2)}) collective-permute-start(f32[2,2,2,128]{3,2,1,0:T(2,128)} %own.1), channel_id=1, source_target_pairs={{2,0},{4,2},{6,4},{8,6},{10,8},{12,10},{14,12},{16,14},{18,16},{20... | collective-permute-start | bytes 12296 | tf_op jit(solution)/shard_map/ppermute | solution.py:214
  9.8 0.7 convert_element_type.8
  10.5 0.9 broadcast_multiply_fusion.weights
  11.4 0.0 copy-start
  11.4 1.9 %collective-permute-start.3 = (f32[128,128]{1,0:T(8,128)S(1)}, f32[128,128]{1,0:T(8,128)S(1)}, u32[]{:S(2)}, u32[]{:S(2)}) collective-permute-start(f32[128,128]{1,0:T(8,128)S(1)} %slice_bitcast_fusion), channel_id=1, source_target_pairs={{0,1},{1,0},{2,3},{3,2},{4,5},{5,4},{6,7},{7,6},{8,9},{9,8},{10,11... | collective-permute-start | bytes 196616 | tf_op jit(solution)/shard_map/ppermute | solution.py:201
  13.4 0.5 multiply_add_fusion.grid
  13.9 0.0 collective-permute-done.before
  13.9 0.0 copy-start.2
  13.9 0.0 collective-permute-done.1.after
  13.9 0.0 copy-start.3
  13.9 0.0 copy-done
  13.9 0.6 copy-done.2
  14.5 0.0 copy-done.3
  14.5 14.1 %chain.1 = (f32[2,2,128,128]{3,2,1,0:T(8,128)}, f32[2,2,128,128]{3,2,1,0:T(8,128)}, f32[2,2,128,128]{3,2,1,0:T(8,128)}, f32[2,2,128,128]{3,2,1,0:T(8,128)}) custom-call(s32[1]{0:T(128)} %bitcast.role, s32[2]{0:T(128)} %shifts.1, f32[2]{0:T(128)} %multiply_add_fusion.grid, f32[2,128,128]{2,1,0:T(8,128)} %ham.1, f32[2,128,128]{2,1,0:T(8,128)} %copy-done, ...), custom_call_target="tpu_custom_call" | custom-call | tf_op jit(solution)/shard_map/chain/pallas_call | solution.py:221
  28.6 2.6 %collective-permute-start.2 = (f32[2,2,128,128]{3,2,1,0:T(8,128)}, f32[2,2,128,128]{3,2,1,0:T(8,128)S(1)}, u32[]{:S(2)}, u32[]{:S(2)}) collective-permute-start(f32[2,2,128,128]{3,2,1,0:T(8,128)} %get-tuple-element.11), channel_id=1, source_target_pairs={{0,1},{1,0},{2,3},{3,2},{4,5},{5,4},{6,7},{7,6},{8,9},{9,8},{10,11... | collective-permute-start | bytes 786440 | tf_op jit(solution)/shard_map/ppermute | solution.py:201
  31.2 0.6 add_divide_fusion.occupation
  31.8 0.0 collective-permute-done.3
  31.8 1.5 %broadcast_select_fusion.w = f32[128,128]{1,0:T(8,128)} fusion(f32[128,128]{1,0:T(8,128)S(1)} %collective-permute-done.3, pred[]{:T(512)S(6)} %eq.3, f32[2,128,128]{2,1,0:T(8,128)} %copy-done), kind=kLoop, calls=%fused_computation.2 | loop fusion | flops 16384 | bytes 196609 | tf_op jit(solution)/shard_map/jit(_where)/select_n | solution.py:217
  33.3 0.0 collective-permute-done.2.received
  33.3 0.0 copy-start.1
  33.3 0.7 copy-done.1
  34.0 9.6 %close.1 = (f32[2,2,2,128,128]{4,3,2,1,0:T(8,128)}, f32[2,128]{1,0:T(2,128)}) custom-call(s32[1]{0:T(128)} %bitcast.role, f32[2]{0:T(128)} %add_divide_fusion.occupation, f32[2,2,128,128]{3,2,1,0:T(8,128)} %get-tuple-element.8.outer_x, f32[2,2,128,128]{3,2,1,0:T(8,128)} %get-tuple-element.9.outer_t, f32[2,2,128,128]{3,2,1,0:T(8,128)} %get-tuple-element.10.inner_s, ...), custom_call_target="tpu_custom_call" | custom-call | tf_op jit(solution)/shard_map/close/pallas_call | solution.py:230
  43.6 0.0 copy-start.4
  43.6 0.7 copy-done.4
  44.3 23.2 %psum.21 = f32[2,128]{1,0:T(2,128)S(1)} all-reduce(f32[2,128]{1,0:T(2,128)S(1)} %copy-done.4), channel_id=1, replica_groups=mesh['energy_0'=8,'energy_1'=8,'energy_2'=4,'slab'=2] {'energy_0'}, use_global_device_ids=true, to_apply=%region_0.1 | all-reduce | flops 256 | bytes 2048 | tf_op jit(solution)/shard_map/psum | solution.py:241
  67.4 14.1 %psum.22 = f32[2,128]{1,0:T(2,128)S(1)} all-reduce(f32[2,128]{1,0:T(2,128)S(1)} %psum.21), channel_id=1, replica_groups=mesh['energy_0'=8,'energy_1'=8,'energy_2'=4,'slab'=2] {'energy_1'}, use_global_device_ids=true, to_apply=%region_1.2 | all-reduce | flops 256 | bytes 2048 | tf_op jit(solution)/shard_map/psum | solution.py:241
  81.6 10.8 %psum.23 = f32[2,128]{1,0:T(2,128)S(1)} all-reduce(f32[2,128]{1,0:T(2,128)S(1)} %psum.22), channel_id=1, replica_groups=mesh['energy_0'=8,'energy_1'=8,'energy_2'=4,'slab'=2] {'energy_2'}, use_global_device_ids=true, to_apply=%region_2.3 | all-reduce | flops 256 | bytes 2048 | tf_op jit(solution)/shard_map/psum | solution.py:241
  92.4 0.6 broadcast_multiply_fusion.1
  (1 shorter events, 0.0 us)
Async XLA Ops:
  0.6 13.3 %collective-permute-start = (f32[2,2,2,128]{3,2,1,0:T(2,128)}, f32[2,2,2,128]{3,2,1,0:T(2,128)S(1)}, u32[]{:S(2)}, u32[]{:S(2)}) collective-permute-start(f32[2,2,2,128]{3,2,1,0:T(2,128)} %own.1), channel_id=1, source_target_pairs={{0,2},{2,4},{4,6},{6,8},{8,10},{10,12},{12,14},{14,16},{16,18},{18... | collective-permute-start | bytes 12296 | tf_op jit(solution)/shard_map/ppermute | solution.py:213
  4.0 9.9 %collective-permute-start.1 = (f32[2,2,2,128]{3,2,1,0:T(2,128)}, f32[2,2,2,128]{3,2,1,0:T(2,128)S(1)}, u32[]{:S(2)}, u32[]{:S(2)}) collective-permute-start(f32[2,2,2,128]{3,2,1,0:T(2,128)} %own.1), channel_id=1, source_target_pairs={{2,0},{4,2},{6,4},{8,6},{10,8},{12,10},{14,12},{16,14},{18,16},{20... | collective-permute-start | bytes 12296 | tf_op jit(solution)/shard_map/ppermute | solution.py:214
  11.4 2.5 %copy-start = (f32[2,128,128]{2,1,0:T(8,128)}, f32[2,128,128]{2,1,0:T(8,128)S(1)}, u32[]{:S(2)}) copy-start(f32[2,128,128]{2,1,0:T(8,128)S(1)} %broadcast_multiply_fusion.weights) | copy-start | bytes 393220
  11.4 20.4 %collective-permute-start.3 = (f32[128,128]{1,0:T(8,128)S(1)}, f32[128,128]{1,0:T(8,128)S(1)}, u32[]{:S(2)}, u32[]{:S(2)}) collective-permute-start(f32[128,128]{1,0:T(8,128)S(1)} %slice_bitcast_fusion), channel_id=1, source_target_pairs={{0,1},{1,0},{2,3},{3,2},{4,5},{5,4},{6,7},{7,6},{8,9},{9,8},{10,11... | collective-permute-start | bytes 196616 | tf_op jit(solution)/shard_map/ppermute | solution.py:201
  13.9 0.6 copy-start.2
  13.9 0.6 copy-start.3
  28.6 4.6 %collective-permute-start.2 = (f32[2,2,128,128]{3,2,1,0:T(8,128)}, f32[2,2,128,128]{3,2,1,0:T(8,128)S(1)}, u32[]{:S(2)}, u32[]{:S(2)}) collective-permute-start(f32[2,2,128,128]{3,2,1,0:T(8,128)} %get-tuple-element.11), channel_id=1, source_target_pairs={{0,1},{1,0},{2,3},{3,2},{4,5},{5,4},{6,7},{7,6},{8,9},{9,8},{10,11... | collective-permute-start | bytes 786440 | tf_op jit(solution)/shard_map/ppermute | solution.py:201
  33.3 0.7 copy-start.1
  43.6 0.7 copy-start.4

commit v2 on v1

--- a/solution.py
+++ b/solution.py
@@ -9,6 +9,7 @@
 from jax.sharding import PartitionSpec as P
 
 ENERGY = ("energy_0", "energy_1", "energy_2")
+MESH = pl.DeviceIdType.MESH
 BROADENING = 0.2
 LEAD_WIDTH = 0.5
 THERMAL = 0.1
@@ -118,29 +119,77 @@
     )
 
 
-def chain(role, shifts, grid, ham, weights, strength, own, before, after, outer_x, outer_t, inner_s, inner_x, real, imag):
+def sweep(
+    ham, coupling, bonds, strength, shifts, own, green_out, density,
+    before, after, near_w, near_b, outer_x, outer_t, inner_s, send_x, recv_x, green, real, imag,
+    partials, line_0, line_1, line_2, halo_send, halo_recv, near_send, near_recv, x_send, x_recv,
+    line_send, line_recv_0, line_recv_1, line_recv_2, out_sem,
+):
     energies, n = own.shape[0], ham.shape[-1]
-    rank = role[0]
+    rank = lax.axis_index("slab")
+    sizes = [lax.axis_size(axis) for axis in ENERGY]
+    place = [lax.axis_index(axis) for axis in ENERGY]
+    devices = sizes[0] * sizes[1] * sizes[2]
+    index = (place[0] * sizes[1] + place[1]) * sizes[2] + place[2]
+
+    def along(step):
+        other = lax.rem(index + step, devices)
+        return (lax.div(other, sizes[1] * sizes[2]), lax.rem(lax.div(other, sizes[2]), sizes[1]), lax.rem(other, sizes[2]), rank)
+
+    following, previous = along(1), along(devices - 1)
+    partner = (*place, 1 - rank)
+    lines = [
+        [(*place[:a], lax.rem(place[a] + step, sizes[a]), *place[a + 1 :], rank) for step in range(1, sizes[a])]
+        for a in range(3)
+    ]
+    barrier = pltpu.get_barrier_semaphore()
+    peers = [following, previous, partner] + lines[0] + lines[1] + lines[2]
+    for peer in peers:
+        pl.semaphore_signal(barrier, inc=1, device_id=peer, device_id_type=MESH)
+
     diagonal = eye(n)
+    w_near = coupling[0] * bonds[0:1, :].astype(jnp.float32)
+    v = coupling[1] * bonds[1:2, :].astype(jnp.float32)
+    v = jnp.where(rank == 0, v, v.T)
+    lead = jnp.where(rank == 0, product(w_near, w_near, ROWS), jnp.where(diagonal, LEAD_WIDTH, 0.0))
+    pl.semaphore_wait(barrier, len(peers))
+
+    def remote(source, target, send, recv, device):
+        return pltpu.make_async_remote_copy(source, target, send, recv, device_id=device, device_id_type=MESH)
+
+    halo = [
+        remote(own, before, halo_send.at[0], halo_recv.at[0], following),
+        remote(own, after, halo_send.at[1], halo_recv.at[1], previous),
+    ]
+    near = [
+        remote(coupling.at[0], near_w, near_send.at[0], near_recv.at[0], partner),
+        remote(bonds, near_b, near_send.at[1], near_recv.at[1], partner),
+    ]
+    for copy in halo + near:
+        copy.start()
+    for copy in halo:
+        copy.wait()
+
+    points = [
+        -HALF_WINDOW + 2.0 * HALF_WINDOW * ((index * energies + e).astype(jnp.float32) + 0.5) / (devices * energies)
+        for e in range(energies)
+    ]
+    has_before, has_after = index > 0, index < devices - 1
 
     def build(slab):
         one = shifts[slab] == 1
-        around = [before.at[e] for e in range(energies)] + [own.at[e] for e in range(energies)]
-        around += [after.at[e] for e in range(energies)]
+        around = [jnp.where(has_before, before[e, slab], 0.0) for e in range(energies)]
+        around += [own[e, slab] for e in range(energies)]
+        around += [jnp.where(has_after, after[e, slab], 0.0) for e in range(energies)]
         blocks = []
         for e in range(energies):
-            at = [around[energies + e + step][slab] for step in (-2, -1, 1, 2)]
-            green = jnp.where(one, at[1] + at[2], at[0] + at[3])
-            self_energy = strength[pl.ds(slab, 1), :] * green
-            re = jnp.where(diagonal, grid[e] - self_energy[0:1, :], 0.0) - ham[slab]
+            far, close, close_up, far_up = [around[energies + e + step] for step in (-2, -1, 1, 2)]
+            self_energy = strength[pl.ds(slab, 1), :] * jnp.where(one, close + close_up, far + far_up)
+            re = jnp.where(diagonal, points[e] - self_energy[0:1, :], 0.0) - ham[slab]
             im = jnp.where(diagonal, BROADENING - self_energy[1:2, :], 0.0)
             blocks.append((re, im))
         return blocks
 
-    w_near = weights[0]
-    v = weights[1]
-    v = jnp.where(rank == 0, v, v.T)
-    lead = jnp.where(rank == 0, product(w_near, w_near, ROWS), jnp.where(diagonal, LEAD_WIDTH, 0.0))
     for e, (re, im) in enumerate(build(rank)):
         real[e] = re
         imag[e] = im + lead
@@ -163,83 +212,96 @@
         imag[e] = im
     invert(real, imag)
     for e in range(energies):
-        inner_x[e, 0] = -real[e]
-        inner_x[e, 1] = -imag[e]
-
-
-def close(role, occupation, outer_x, outer_t, inner_s, received, w, green, density, real, imag):
-    energies, n = outer_x.shape[0], w.shape[-1]
-    rank = role[0]
-    diagonal = eye(n)
-    u = w[...]
-    u = jnp.where(rank == 0, u.T, u)
+        send_x[e, 0] = -real[e]
+        send_x[e, 1] = -imag[e]
+    swap = remote(send_x, recv_x, x_send.at[0], x_recv.at[0], partner)
+    swap.start()
+    for copy in near:
+        copy.wait()
+    theirs = near_w[...] * near_b[0:1, :].astype(jnp.float32)
+    u = jnp.where(rank == 0, theirs.T, w_near)
+    swap.wait()
     for e in range(energies):
-        t = product(jnp.concatenate([received[e, 0], received[e, 1]], axis=0), u)
+        t = product(jnp.concatenate([recv_x[e, 0], recv_x[e, 1]], axis=0), u)
         self_energy = product(u, jnp.concatenate([t[:n], t[n:]], axis=1), ROWS)
         real[e] = inner_s[e, 0] - self_energy[:, :n]
         imag[e] = inner_s[e, 1] - self_energy[:, n:]
     invert(real, imag)
     inner_sum = jnp.zeros((1, n), jnp.float32)
     outer_sum = jnp.zeros((1, n), jnp.float32)
+    stores = []
     for e in range(energies):
         gr, gi = -real[e], -imag[e]
         green[e, 1 - rank, 0] = gr
         green[e, 1 - rank, 1] = gi
         tr, ti = outer_t[e, 0], outer_t[e, 1]
         y = product(jnp.concatenate([tr, ti], axis=1), pair(gr, gi))
-        z = product(y, jnp.concatenate([jnp.concatenate([tr, -ti], axis=1), jnp.concatenate([ti, tr], axis=1)], axis=0), COLUMNS)
-        or_, oi = outer_x[e, 0] + z[:, :n], outer_x[e, 1] + z[:, n:]
-        green[e, rank, 0] = or_
-        green[e, rank, 1] = oi
-        inner_sum += occupation[e] * jnp.sum(jnp.where(diagonal, gi, 0.0), axis=0, keepdims=True)
-        outer_sum += occupation[e] * jnp.sum(jnp.where(diagonal, oi, 0.0), axis=0, keepdims=True)
-    density[pl.ds(rank, 1), :] = outer_sum
-    density[pl.ds(1 - rank, 1), :] = inner_sum
-
-
-def exchange(x):
-    return lax.ppermute(x, "slab", [(0, 1), (1, 0)])
+        turned = jnp.concatenate([jnp.concatenate([tr, -ti], axis=1), jnp.concatenate([ti, tr], axis=1)], axis=0)
+        z = product(y, turned, COLUMNS)
+        re, im = outer_x[e, 0] + z[:, :n], outer_x[e, 1] + z[:, n:]
+        green[e, rank, 0] = re
+        green[e, rank, 1] = im
+        occupied = 1.0 / (1.0 + jnp.exp(jnp.full((1, n), points[e] / THERMAL, jnp.float32)))
+        inner_sum += occupied * jnp.sum(jnp.where(diagonal, gi, 0.0), axis=0, keepdims=True)
+        outer_sum += occupied * jnp.sum(jnp.where(diagonal, im, 0.0), axis=0, keepdims=True)
+    partials[0, pl.ds(rank, 1), :] = outer_sum
+    partials[0, pl.ds(1 - rank, 1), :] = inner_sum
+    store = pltpu.make_async_copy(green, green_out, out_sem.at[0])
+    store.start()
+    buffers = [line_0, line_1, line_2]
+    arrivals = [line_recv_0, line_recv_1, line_recv_2]
+    for stage, a in enumerate((2, 1, 0)):
+        buffer, arrival, mine = buffers[a], arrivals[a], place[a]
+        source = partials.at[stage]
+        copies = [
+            remote(source, buffer.at[mine], line_send.at[a, step], arrival.at[mine], device)
+            for step, device in enumerate(lines[a])
+        ]
+        for copy in copies:
+            copy.start()
+        buffer[mine] = partials[stage]
+        for step in range(1, sizes[a]):
+            sender = lax.rem(mine + step, sizes[a])
+            remote(source, buffer.at[sender], line_send.at[a, step - 1], arrival.at[sender], lines[a][step - 1]).wait_recv()
+        total = buffer[0]
+        for other in range(1, sizes[a]):
+            total = total + buffer[other]
+        if stage < 2:
+            partials[stage + 1] = total
+        else:
+            density[...] = (-2.0 * HALF_WINDOW / (devices * energies) / jnp.pi) * total
+        for copy in copies:
+            copy.wait_send()
+    store.wait()
 
 
 def shards(hamiltonian, coupling, bonds, phonon_coupling, previous_green, phonon_shift):
-    energies, n = previous_green.shape[0], hamiltonian.shape[1]
-    rank = lax.axis_index("slab")
-    size = lax.axis_size(ENERGY)
-    total = energies * size
-    first = lax.axis_index(ENERGY) * energies
-    points = (jnp.arange(energies, dtype=jnp.int32) + first).astype(jnp.float32) + 0.5
-    grid = -HALF_WINDOW + 2.0 * HALF_WINDOW * points / total
-    up = [(i, i + 1) for i in range(size - 1)]
-    before = lax.ppermute(previous_green, ENERGY, up)
-    after = lax.ppermute(previous_green, ENERGY, [(j, i) for i, j in up])
-    weights = coupling * bonds[:, None, :].astype(jnp.float32)
-    theirs = exchange(weights[0])
-    middle = jnp.where(rank == 0, theirs, weights[0])
-    role = jnp.reshape(rank, (1,)).astype(jnp.int32)
-    block = jax.ShapeDtypeStruct((energies, 2, n, n), jnp.float32)
-    scratch = [pltpu.VMEM((energies, n, n), jnp.float32)] * 2
-    outer_x, outer_t, inner_s, inner_x = pl.pallas_call(
-        chain,
-        out_shape=[block] * 4,
-        in_specs=[SMEM] * 3 + [VMEM] * 6,
-        out_specs=[VMEM] * 4,
-        scratch_shapes=scratch,
-        name="chain",
-    )(role, phonon_shift, grid, hamiltonian, weights, phonon_coupling, previous_green, before, after)
-    received = exchange(inner_x)
-    green, partial = pl.pallas_call(
-        close,
-        out_shape=[
-            jax.ShapeDtypeStruct((energies, 2, 2, n, n), jnp.float32),
-            jax.ShapeDtypeStruct((2, n), jnp.float32),
+    energies, slabs, n = previous_green.shape[0], hamiltonian.shape[0], hamiltonian.shape[1]
+    sizes = [lax.axis_size(axis) for axis in ENERGY]
+    longest = max(sizes)
+    block = pltpu.VMEM((energies, 2, n, n), jnp.float32)
+    square = pltpu.VMEM((energies, n, n), jnp.float32)
+    halo = pltpu.VMEM(previous_green.shape, jnp.float32)
+    dma = pltpu.SemaphoreType.DMA
+    return pl.pallas_call(
+        sweep,
+        out_shape=(
+            jax.ShapeDtypeStruct((energies, slabs, 2, n, n), jnp.float32),
+            jax.ShapeDtypeStruct((slabs, n), jnp.float32),
+        ),
+        in_specs=[VMEM] * 4 + [SMEM, VMEM],
+        out_specs=(pl.BlockSpec(memory_space=pl.ANY), VMEM),
+        scratch_shapes=[
+            halo, halo, pltpu.VMEM((n, n), jnp.float32), pltpu.VMEM(bonds.shape, jnp.int32),
+            block, block, block, block, block, pltpu.VMEM((energies, slabs, 2, n, n), jnp.float32), square, square,
+            pltpu.VMEM((3, slabs, n), jnp.float32),
+            *[pltpu.VMEM((size, slabs, n), jnp.float32) for size in sizes],
+            dma((2,)), dma((2,)), dma((2,)), dma((2,)), dma((1,)), dma((1,)),
+            dma((3, longest)), *[dma((size,)) for size in sizes], dma((1,)),
         ],
-        in_specs=[SMEM] * 2 + [VMEM] * 5,
-        out_specs=[VMEM] * 2,
-        scratch_shapes=scratch,
-        name="close",
-    )(role, jax.nn.sigmoid(-grid / THERMAL), outer_x, outer_t, inner_s, received, middle)
-    summed = functools.reduce(lax.psum, ENERGY, partial)
-    return green, -2.0 * HALF_WINDOW / total / jnp.pi * summed
+        compiler_params=pltpu.CompilerParams(collective_id=0, has_side_effects=True),
+        name="sweep",
+    )(hamiltonian, coupling, bonds, phonon_coupling, phonon_shift, previous_green)
 
 
 def solution(mesh):

time: 93.3 us -> 56.6 us (0.61)
  the two profiles are of different devices: /device:TPU:32 before, /device:TPU:8 now
where the time goes in v2:
time: 56.6 us; the launch traced here: 56.5 us
  Pallas kernels  53.4 us (94%)
  local copies, waits for them, and re-layouts  2.44 us (4%)
  between operations  0.65 us (1%)
    pallas_call x1, Pallas kernels, shards(): pl.pallas_call(sweep, out_shape=(jax.ShapeDtypeStruct((energies, slabs, 2...  53.4 us
    unnamed x4, local copies, waits for them, and re-layouts  2.44 us

profile of v2, /device:TPU:8, one launch (start us, length us, event | category | flops | bytes accessed | tf_op | source)
XLA Modules:
  0.0 56.5 jit_solution(1220507348671150946)
XLA Ops:
  0.6 53.4 %sweep.1 = (f32[2,2,2,128,128]{4,3,2,1,0:T(8,128)}, f32[2,128]{1,0:T(2,128)}) custom-call(f32[2,128,128]{2,1,0:T(8,128)} %ham.1, f32[2,128,128]{2,1,0:T(8,128)} %coupling.1, s32[2,128]{1,0:T(2,128)} %bonds.1, f32[2,128]{1,0:T(2,128)} %strength.1, s32[2]{0:T(128)} %shifts.1, f32[2,2,2,128]{3,2,1,0:T(2,128)} %own.1), custom_call_target="tpu_custom_call" | custom-call | tf_op jit(solution)/shard_map/sweep/pallas_call | solution.py:286
  54.0 0.0 copy-start
  54.0 1.9 %copy.10 = f32[2,2,2,128,128]{4,3,2,1,0:T(8,128)} copy(f32[2,2,2,128,128]{4,3,2,1,0:T(8,128)} %get-tuple-element.4) | data formatting | bytes 1048576
  55.9 0.0 copy-done
  55.9 0.6 copy.11
Async XLA Ops:
  54.0 1.9 %copy-start = (f32[2,128]{1,0:T(2,128)S(1)}, f32[2,128]{1,0:T(2,128)}, u32[]{:S(2)}) copy-start(f32[2,128]{1,0:T(2,128)} %get-tuple-element.5) | copy-start | bytes 3076

commit v3 on v2

v3 whole, which is shorter than its diff:
```python
import functools

import jax
import jax.numpy as jnp
from jax import lax
from jax.experimental import pallas as pl
from jax.experimental.pallas import tpu as pltpu
from jax.sharding import Mesh
from jax.sharding import PartitionSpec as P

ENERGY = ("energy_0", "energy_1", "energy_2")
MESH = pl.DeviceIdType.MESH
BROADENING = 0.2
LEAD_WIDTH = 0.5
THERMAL = 0.1
HALF_WINDOW = 3.0
GROUP = 8
PANEL = 16
ROWS = (((0,), (0,)), ((), ()))
PLAIN = (((1,), (0,)), ((), ()))
COLUMNS = (((1,), (1,)), ((), ()))
VMEM = pl.BlockSpec(memory_space=pltpu.VMEM)
HBM = pl.BlockSpec(memory_space=pltpu.HBM)


def split(x):
    high = x.astype(jnp.bfloat16)
    return high, (x - high.astype(jnp.float32)).astype(jnp.bfloat16)


def dot(left, right, dims=PLAIN):
    return lax.dot_general(left, right, dims, preferred_element_type=jnp.float32)


def product(left, right, dims=PLAIN):
    (lh, ll), (rh, rl) = split(left), split(right)
    return dot(lh, rh, dims) + (dot(ll, rh, dims) + dot(lh, rl, dims))


def eye(n):
    return lax.broadcasted_iota(jnp.int32, (n, n), 0) == lax.broadcasted_iota(jnp.int32, (n, n), 1)


def times(a, b):
    return a[0] * b[0] - a[1] * b[1], a[0] * b[1] + a[1] * b[0]


def minus(a, b):
    return a[0] - b[0], a[1] - b[1]


def spread(x, k):
    return tuple(jnp.broadcast_to(part[k : k + 1, :], part.shape) for part in x)


def total_of(parts):
    while len(parts) > 1:
        parts = [parts[i] + parts[i + 1] for i in range(0, len(parts), 2)]
    return parts[0]


def eliminate(panels, first):
    energies, count = range(len(panels)), len(panels[0])
    shape = panels[0][0][0].shape
    lane = lax.broadcasted_iota(jnp.int32, shape, 1)
    row = lax.broadcasted_iota(jnp.int32, shape, 0)

    def column(x, j):
        return tuple(
            jnp.broadcast_to(jnp.sum(jnp.where(lane == j, part, 0.0), axis=1, keepdims=True), shape) for part in x
        )

    for g in range(count):
        start = first + g * GROUP
        inside = (lane >= start) & (lane < start + GROUP)
        unit = jnp.where(lane == start + row, 1.0, 0.0)
        others = [(g + t) % count for t in range(1, count)]
        pivots = [[column(panels[e][g], start + k) for k in range(GROUP)] for e in energies]
        solved = [
            (jnp.where(inside, unit, panels[e][g][0]), jnp.where(inside, 0.0, panels[e][g][1])) for e in energies
        ]
        columns = [{h: [column(panels[e][h], start + k) for k in range(GROUP)] for h in others} for e in energies]
        for k in range(GROUP):
            for e in energies:
                c = pivots[e][k]
                p = spread(c, k)
                d = 1.0 / (p[0] * p[0] + p[1] * p[1])
                q = (p[0] * d, -(p[1] * d))
                w = times(c, q)
                w = (jnp.where(row == k, 1.0 - q[0], w[0]), jnp.where(row == k, -q[1], w[1]))
                for j in range(k + 1, GROUP):
                    pivots[e][j] = minus(pivots[e][j], times(w, spread(pivots[e][j], k)))
                solved[e] = minus(solved[e], times(w, spread(solved[e], k)))
        for e in energies:
            panels[e][g] = solved[e]
            lines = [spread(solved[e], k) for k in range(GROUP)]
            for h in others:
                terms = [times(columns[e][h][k], lines[k]) for k in range(GROUP)]
                rest = tuple(jnp.where(inside, 0.0, part) for part in panels[e][h])
                panels[e][h] = minus(rest, (total_of([t[0] for t in terms]), total_of([t[1] for t in terms])))
    return panels


def invert(real, imag):
    energies, n = real.shape[0], real.shape[-1]
    lane = lax.broadcasted_iota(jnp.int32, (PANEL, n), 1)
    for first in range(0, n, PANEL):
        inside = (lane >= first) & (lane < first + PANEL)
        before, panels = [], []
        for e in range(energies):
            before.append(jnp.concatenate([real[e, first : first + PANEL, :], imag[e, first : first + PANEL, :]], axis=0))
            panels.append(
                [(real[e, at : at + GROUP, :], imag[e, at : at + GROUP, :]) for at in range(first, first + PANEL, GROUP)]
            )
        panels = eliminate(panels, first)
        for e in range(energies):
            tr = jnp.concatenate([x for x, _ in panels[e]], axis=0)
            ti = jnp.concatenate([y for _, y in panels[e]], axis=0)
            tr, ti = jnp.where(inside, -tr, tr), jnp.where(inside, -ti, ti)
            (lh, ll), (rh, rl), (ih, il) = split(before[e]), split(tr), split(ti)
            high, low = pair(rh, ih), pair(rl, il)
            update = dot(
                jnp.concatenate([lh, ll, lh, ll], axis=0), jnp.concatenate([high, high, low, low], axis=0), ROWS
            )
            for at in range(0, n, PANEL):
                s = slice(at, at + PANEL)
                if at == first:
                    real[e, s, :], imag[e, s, :] = tr, ti
                else:
                    real[e, s, :] = jnp.where(inside, 0.0, real[e, s, :]) - update[s, :n]
                    imag[e, s, :] = jnp.where(inside, 0.0, imag[e, s, :]) - update[s, n:]


def pair(real, imag):
    return jnp.concatenate(
        [jnp.concatenate([real, imag], axis=1), jnp.concatenate([-imag, real], axis=1)], axis=0
    )


def sweep(
    ham_in, coupling_in, bonds_in, strength_in, shifts_in, own_in, green, density,
    ham, coupling, bonds, strength, shifts, own, before, after, near_w, near_b, outer_x, outer_u, inner_s, send_x, recv_x, real, imag,
    partials, line_0, line_1, line_2, halo_send, halo_recv, near_send, near_recv, x_send, x_recv,
    line_send, line_recv_0, line_recv_1, line_recv_2, load_sem,
):
    loads = [
        pltpu.make_async_copy(source, target, load_sem.at[i])
        for i, (source, target) in enumerate(
            ((coupling_in, coupling), (bonds_in, bonds), (own_in, own), (strength_in, strength), (shifts_in, shifts), (ham_in, ham))
        )
    ]
    for load in loads:
        load.start()
    energies, n = own.shape[0], ham.shape[-1]
    rank = lax.axis_index("slab")
    sizes = [lax.axis_size(axis) for axis in ENERGY]
    place = [lax.axis_index(axis) for axis in ENERGY]
    devices = sizes[0] * sizes[1] * sizes[2]
    index = (place[0] * sizes[1] + place[1]) * sizes[2] + place[2]

    def along(step):
        other = lax.rem(index + step, devices)
        return (lax.div(other, sizes[1] * sizes[2]), lax.rem(lax.div(other, sizes[2]), sizes[1]), lax.rem(other, sizes[2]), rank)

    following, previous = along(1), along(devices - 1)
    partner = (*place, 1 - rank)
    lines = [
        [(*place[:a], lax.rem(place[a] + step, sizes[a]), *place[a + 1 :], rank) for step in range(1, sizes[a])]
        for a in range(3)
    ]
    barrier = pltpu.get_barrier_semaphore()
    peers = [following, previous, partner] + lines[0] + lines[1] + lines[2]
    for peer in peers:
        pl.semaphore_signal(barrier, inc=1, device_id=peer, device_id_type=MESH)

    diagonal = eye(n)
    for load in loads[:2]:
        load.wait()
    w_near = coupling[0] * bonds[0:1, :].astype(jnp.float32)
    v = coupling[1] * bonds[1:2, :].astype(jnp.float32)
    v = jnp.where(rank == 0, v, v.T)
    lead = jnp.where(rank == 0, product(w_near, w_near, ROWS), jnp.where(diagonal, LEAD_WIDTH, 0.0))
    pl.semaphore_wait(barrier, len(peers))

    def remote(source, target, send, recv, device):
        return pltpu.make_async_remote_copy(source, target, send, recv, device_id=device, device_id_type=MESH)

    halo = [
        remote(own_in, before, halo_send.at[0], halo_recv.at[0], following),
        remote(own_in, after, halo_send.at[1], halo_recv.at[1], previous),
    ]
    near = [
        remote(coupling_in.at[0], near_w, near_send.at[0], near_recv.at[0], partner),
        remote(bonds_in, near_b, near_send.at[1], near_recv.at[1], partner),
    ]
    for copy in halo + near:
        copy.start()
    for load in loads[2:]:
        load.wait()
    for copy in halo:
        copy.wait()

    points = [
        -HALF_WINDOW + 2.0 * HALF_WINDOW * ((index * energies + e).astype(jnp.float32) + 0.5) / (devices * energies)
        for e in range(energies)
    ]
    has_before, has_after = index > 0, index < devices - 1

    def build(slab):
        one = shifts[slab] == 1
        around = [jnp.where(has_before, before[e, slab], 0.0) for e in range(energies)]
        around += [own[e, slab] for e in range(energies)]
        around += [jnp.where(has_after, after[e, slab], 0.0) for e in range(energies)]
        blocks = []
        for e in range(energies):
            far, close, close_up, far_up = [around[energies + e + step] for step in (-2, -1, 1, 2)]
            self_energy = strength[pl.ds(slab, 1), :] * jnp.where(one, close + close_up, far + far_up)
            re = jnp.where(diagonal, points[e] - self_energy[0:1, :], 0.0) - ham[slab]
            im = jnp.where(diagonal, BROADENING - self_energy[1:2, :], 0.0)
            blocks.append((re, im))
        return blocks

    for e, (re, im) in enumerate(build(rank)):
        real[e] = re
        imag[e] = im + lead
    invert(real, imag)
    inner = build(1 - rank)
    for e in range(energies):
        xr, xi = -real[e], -imag[e]
        outer_x[e, 0] = xr
        outer_x[e, 1] = xi
        t = product(v, jnp.concatenate([xr, xi], axis=1), ROWS)
        outer_u[e, 0] = t[:, :n]
        outer_u[e, 1] = t[:, n:]
        self_energy = product(jnp.concatenate([t[:, :n], t[:, n:]], axis=0), v)
        re = inner[e][0] - self_energy[:n]
        im = inner[e][1] - self_energy[n:]
        inner_s[e, 0] = re
        inner_s[e, 1] = im
        real[e] = re
        imag[e] = im
    invert(real, imag)
    for e in range(energies):
        send_x[e, 0] = -real[e]
        send_x[e, 1] = -imag[e]
    swap = remote(send_x, recv_x, x_send.at[0], x_recv.at[0], partner)
    swap.start()
    for copy in near:
        copy.wait()
    theirs = near_w[...] * near_b[0:1, :].astype(jnp.float32)
    u = jnp.where(rank == 0, theirs.T, w_near)
    swap.wait()
    for e in range(energies):
        t = product(jnp.concatenate([recv_x[e, 0], recv_x[e, 1]], axis=0), u)
        self_energy = product(u, jnp.concatenate([t[:n], t[n:]], axis=1), ROWS)
        real[e] = inner_s[e, 0] - self_energy[:, :n]
        imag[e] = inner_s[e, 1] - self_energy[:, n:]
    invert(real, imag)
    sums = [jnp.zeros((1, n), jnp.float32), jnp.zeros((1, n), jnp.float32)]
    halves = []
    for e in range(energies):
        gr, gi = -real[e], -imag[e]
        ur, ui = outer_u[e, 0], outer_u[e, 1]
        y = product(jnp.concatenate([gr, gi], axis=0), jnp.concatenate([ur, ui], axis=1))
        yr, yi = y[:n, :n] - y[n:, n:], y[:n, n:] + y[n:, :n]
        halves.append((yr, yi))
        outer = outer_x[e, 1] * jnp.where(diagonal, 1.0, 0.0) + (ur * yi + ui * yr)
        occupied = 1.0 / (1.0 + jnp.exp(jnp.full((1, n), points[e] / THERMAL, jnp.float32)))
        sums[0] += occupied * jnp.sum(outer, axis=0, keepdims=True)
        sums[1] += occupied * jnp.sum(jnp.where(diagonal, gi, 0.0), axis=0, keepdims=True)
    partials[0, pl.ds(rank, 1), :] = sums[0]
    partials[0, pl.ds(1 - rank, 1), :] = sums[1]

    def finish():
        for e in range(energies):
            green[e, 1 - rank, 0] = -real[e]
            green[e, 1 - rank, 1] = -imag[e]
            yr, yi = halves[e]
            ur, ui = outer_u[e, 0], outer_u[e, 1]
            left = jnp.concatenate([jnp.concatenate([ur, ui], axis=1), jnp.concatenate([-ui, ur], axis=1)], axis=0)
            z = product(left, jnp.concatenate([yr, yi], axis=0), ROWS)
            green[e, rank, 0] = outer_x[e, 0] + z[:n]
            green[e, rank, 1] = outer_x[e, 1] + z[n:]

    buffers = [line_0, line_1, line_2]
    arrivals = [line_recv_0, line_recv_1, line_recv_2]
    for stage, a in enumerate((2, 1, 0)):
        buffer, arrival, mine = buffers[a], arrivals[a], place[a]
        source = partials.at[stage]
        copies = [
            remote(source, buffer.at[mine], line_send.at[a, step], arrival.at[mine], device)
            for step, device in enumerate(lines[a])
        ]
        for copy in copies:
            copy.start()
        buffer[mine] = partials[stage]
        if stage == 0:
            finish()
        for step in range(1, sizes[a]):
            sender = lax.rem(mine + step, sizes[a])
            remote(source, buffer.at[sender], line_send.at[a, step - 1], arrival.at[sender], lines[a][step - 1]).wait_recv()
        total = buffer[0]
        for other in range(1, sizes[a]):
            total = total + buffer[other]
        if stage < 2:
            partials[stage + 1] = total
        else:
            density[...] = (-2.0 * HALF_WINDOW / (devices * energies) / jnp.pi) * total
        for copy in copies:
            copy.wait_send()


def shards(hamiltonian, coupling, bonds, phonon_coupling, previous_green, phonon_shift):
    energies, slabs, n = previous_green.shape[0], hamiltonian.shape[0], hamiltonian.shape[1]
    sizes = [lax.axis_size(axis) for axis in ENERGY]
    longest = max(sizes)
    block = pltpu.VMEM((energies, 2, n, n), jnp.float32)
    square = pltpu.VMEM((energies, n, n), jnp.float32)
    halo = pltpu.VMEM(previous_green.shape, jnp.float32)
    dma = pltpu.SemaphoreType.DMA
    return pl.pallas_call(
        sweep,
        out_shape=(
            jax.ShapeDtypeStruct((energies, slabs, 2, n, n), jnp.float32),
            jax.ShapeDtypeStruct((slabs, n), jnp.float32),
        ),
        in_specs=[HBM] * 6,
        out_specs=(VMEM, VMEM),
        scratch_shapes=[
            *[pltpu.VMEM(x.shape, x.dtype) for x in (hamiltonian, coupling, bonds, phonon_coupling)],
            pltpu.SMEM(phonon_shift.shape, jnp.int32), halo, halo, halo, pltpu.VMEM((n, n), jnp.float32), pltpu.VMEM(bonds.shape, jnp.int32),
            block, block, block, block, block, square, square,
            pltpu.VMEM((3, slabs, n), jnp.float32),
            *[pltpu.VMEM((size, slabs, n), jnp.float32) for size in sizes],
            dma((2,)), dma((2,)), dma((2,)), dma((2,)), dma((1,)), dma((1,)),
            dma((3, longest)), *[dma((size,)) for size in sizes], dma((6,)),
        ],
        compiler_params=pltpu.CompilerParams(collective_id=0, has_side_effects=True, vmem_limit_bytes=16 << 20),
        name="sweep",
    )(*[
        pltpu.with_memory_space_constraint(x, pltpu.HBM)
        for x in (hamiltonian, coupling, bonds, phonon_coupling, phonon_shift, previous_green)
    ])


def solution(mesh):
    split_mesh = Mesh(mesh.devices.reshape(8, 8, 4, mesh.shape["slab"]), (*ENERGY, "slab"))
    in_specs = (
        P("slab", None, None),
        P("slab", None, None),
        P("slab", None),
        P("slab", None),
        P(ENERGY, "slab", None, None),
        P("slab"),
    )
    out_specs = (P(ENERGY, "slab", None, None, None), P("slab", None))
    return jax.shard_map(shards, mesh=split_mesh, in_specs=in_specs, out_specs=out_specs, check_vma=False)
```

time: 56.6 us -> 51.3 us (0.906)
  Pallas kernels: 53.4 us -> 49.2 us
  local copies, waits for them, and re-layouts: 2.44 us -> 1.36 us
    pallas_call x1, Pallas kernels: 53.4 us -> 49.2 us  [shards(): pl.pallas_call(sweep, out_shape=(jax.ShapeDtypeStruct((energies, slabs, 2...]
    unnamed x4 -> x2, local copies, waits for them, and re-layouts: 2.44 us -> 1.36 us
where the time goes in v3:
time: 51.3 us; the launch traced here: 51.2 us
  Pallas kernels  49.2 us (96%)
  local copies, waits for them, and re-layouts  1.36 us (3%)
  between operations  0.64 us (1%)
    pallas_call x1, Pallas kernels, shards(): pl.pallas_call(sweep, out_shape=(jax.ShapeDtypeStruct((energies, slabs, 2...  49.2 us
    unnamed x2, local copies, waits for them, and re-layouts  1.36 us

profile of v3, /device:TPU:8, one launch (start us, length us, event | category | flops | bytes accessed | tf_op | source)
XLA Modules:
  0.0 51.2 jit_solution(17634571589419441590)
XLA Ops:
  0.6 49.2 %sweep.1 = (f32[2,2,2,128,128]{4,3,2,1,0:T(8,128)S(1)}, f32[2,128]{1,0:T(2,128)S(1)}) custom-call(f32[2,128,128]{2,1,0:T(8,128)} %ham_in.1, f32[2,128,128]{2,1,0:T(8,128)} %coupling_in.1, s32[2,128]{1,0:T(2,128)} %bonds_in.1, f32[2,128]{1,0:T(2,128)} %strength_in.1, s32[2]{0:T(128)} %shifts_in.1, f32[2,2,2,128]{3,2,1,0:T(2,128)} %own_in.1), custom_call_target="tpu_custom_call" | custom-call | tf_op jit(solution)/shard_map/sweep/pallas_call | solution.py:321
  49.8 0.8 %copy.10 = f32[2,2,2,128,128]{4,3,2,1,0:T(8,128)} copy(f32[2,2,2,128,128]{4,3,2,1,0:T(8,128)S(1)} %get-tuple-element.4) | data formatting | bytes 1048576
  50.6 0.6 %copy.11 = f32[2,128]{1,0:T(2,128)} copy(f32[2,128]{1,0:T(2,128)S(1)} %get-tuple-element.5) | data formatting | bytes 2048

commit v4 on v3

--- a/solution.py
+++ b/solution.py
@@ -15,7 +15,6 @@
 THERMAL = 0.1
 HALF_WINDOW = 3.0
 GROUP = 8
-PANEL = 16
 ROWS = (((0,), (0,)), ((), ()))
 PLAIN = (((1,), (0,)), ((), ()))
 COLUMNS = (((1,), (1,)), ((), ()))
@@ -28,6 +27,14 @@
     return high, (x - high.astype(jnp.float32)).astype(jnp.bfloat16)
 
 
+def thirds(x):
+    parts = []
+    for _ in range(3):
+        parts.append(x.astype(jnp.bfloat16))
+        x = x - parts[-1].astype(jnp.float32)
+    return parts
+
+
 def dot(left, right, dims=PLAIN):
     return lax.dot_general(left, right, dims, preferred_element_type=jnp.float32)
 
@@ -59,9 +66,9 @@
     return parts[0]
 
 
-def eliminate(panels, first):
-    energies, count = range(len(panels)), len(panels[0])
-    shape = panels[0][0][0].shape
+def invert(real, imag):
+    energies, n = range(real.shape[0]), real.shape[-1]
+    shape = (GROUP, n)
     lane = lax.broadcasted_iota(jnp.int32, shape, 1)
     row = lax.broadcasted_iota(jnp.int32, shape, 0)
 
@@ -70,16 +77,20 @@
             jnp.broadcast_to(jnp.sum(jnp.where(lane == j, part, 0.0), axis=1, keepdims=True), shape) for part in x
         )
 
-    for g in range(count):
-        start = first + g * GROUP
-        inside = (lane >= start) & (lane < start + GROUP)
-        unit = jnp.where(lane == start + row, 1.0, 0.0)
-        others = [(g + t) % count for t in range(1, count)]
-        pivots = [[column(panels[e][g], start + k) for k in range(GROUP)] for e in energies]
-        solved = [
-            (jnp.where(inside, unit, panels[e][g][0]), jnp.where(inside, 0.0, panels[e][g][1])) for e in energies
-        ]
-        columns = [{h: [column(panels[e][h], start + k) for k in range(GROUP)] for h in others} for e in energies]
+    def load(e, at):
+        return real[e, at : at + GROUP, :], imag[e, at : at + GROUP, :]
+
+    current = [load(e, 0) for e in energies]
+    for first in range(0, n, GROUP):
+        inside = (lane >= first) & (lane < first + GROUP)
+        unit = jnp.where(lane == first + row, 1.0, 0.0)
+        before = current
+        pivots = [[column(before[e], first + k) for k in range(GROUP)] for e in energies]
+        solved = [(jnp.where(inside, unit, before[e][0]), jnp.where(inside, 0.0, before[e][1])) for e in energies]
+        second = first + GROUP
+        if second < n:
+            following = [load(e, second) for e in energies]
+            columns = [[column(following[e], first + k) for k in range(GROUP)] for e in energies]
         for k in range(GROUP):
             for e in energies:
                 c = pivots[e][k]
@@ -91,44 +102,26 @@
                 for j in range(k + 1, GROUP):
                     pivots[e][j] = minus(pivots[e][j], times(w, spread(pivots[e][j], k)))
                 solved[e] = minus(solved[e], times(w, spread(solved[e], k)))
+        current = []
         for e in energies:
-            panels[e][g] = solved[e]
-            lines = [spread(solved[e], k) for k in range(GROUP)]
-            for h in others:
-                terms = [times(columns[e][h][k], lines[k]) for k in range(GROUP)]
-                rest = tuple(jnp.where(inside, 0.0, part) for part in panels[e][h])
-                panels[e][h] = minus(rest, (total_of([t[0] for t in terms]), total_of([t[1] for t in terms])))
-    return panels
-
-
-def invert(real, imag):
-    energies, n = real.shape[0], real.shape[-1]
-    lane = lax.broadcasted_iota(jnp.int32, (PANEL, n), 1)
-    for first in range(0, n, PANEL):
-        inside = (lane >= first) & (lane < first + PANEL)
-        before, panels = [], []
-        for e in range(energies):
-            before.append(jnp.concatenate([real[e, first : first + PANEL, :], imag[e, first : first + PANEL, :]], axis=0))
-            panels.append(
-                [(real[e, at : at + GROUP, :], imag[e, at : at + GROUP, :]) for at in range(first, first + PANEL, GROUP)]
+            swept = tuple(jnp.where(inside, -part, part) for part in solved[e])
+            if second < n:
+                terms = [times(columns[e][k], spread(swept, k)) for k in range(GROUP)]
+                rest = tuple(jnp.where(inside, 0.0, part) for part in following[e])
+                current.append(minus(rest, (total_of([t[0] for t in terms]), total_of([t[1] for t in terms]))))
+            left = thirds(jnp.concatenate(before[e], axis=0))
+            right = [pair(x, y) for x, y in zip(thirds(swept[0] + unit), thirds(swept[1]))]
+            which = ((0, 0), (1, 0), (2, 0), (0, 1), (1, 1), (0, 2))
+            update = dot(
+                jnp.concatenate([left[i] for i, _ in which], axis=0),
+                jnp.concatenate([right[j] for _, j in which], axis=0),
+                ROWS,
             )
-        panels = eliminate(panels, first)
-        for e in range(energies):
-            tr = jnp.concatenate([x for x, _ in panels[e]], axis=0)
-            ti = jnp.concatenate([y for _, y in panels[e]], axis=0)
-            tr, ti = jnp.where(inside, -tr, tr), jnp.where(inside, -ti, ti)
-            (lh, ll), (rh, rl), (ih, il) = split(before[e]), split(tr), split(ti)
-            high, low = pair(rh, ih), pair(rl, il)
-            update = dot(
-                jnp.concatenate([lh, ll, lh, ll], axis=0), jnp.concatenate([high, high, low, low], axis=0), ROWS
-            )
-            for at in range(0, n, PANEL):
-                s = slice(at, at + PANEL)
-                if at == first:
-                    real[e, s, :], imag[e, s, :] = tr, ti
-                else:
-                    real[e, s, :] = jnp.where(inside, 0.0, real[e, s, :]) - update[s, :n]
-                    imag[e, s, :] = jnp.where(inside, 0.0, imag[e, s, :]) - update[s, n:]
+            for at in [*range(second + GROUP, n, GROUP), *range(0, first, GROUP)]:
+                s = slice(at, at + GROUP)
+                real[e, s, :] = real[e, s, :] - update[s, :n]
+                imag[e, s, :] = imag[e, s, :] - update[s, n:]
+            real[e, first:second, :], imag[e, first:second, :] = swept
 
 
 def pair(real, imag):
@@ -173,6 +166,21 @@
     for peer in peers:
         pl.semaphore_signal(barrier, inc=1, device_id=peer, device_id_type=MESH)
 
+    pl.semaphore_wait(barrier, len(peers))
+
+    def remote(source, target, send, recv, device):
+        return pltpu.make_async_remote_copy(source, target, send, recv, device_id=device, device_id_type=MESH)
+
+    halo = [
+        remote(own_in, before, halo_send.at[0], halo_recv.at[0], following),
+        remote(own_in, after, halo_send.at[1], halo_recv.at[1], previous),
+    ]
+    near = [
+        remote(coupling_in.at[0], near_w, near_send.at[0], near_recv.at[0], partner),
+        remote(bonds_in, near_b, near_send.at[1], near_recv.at[1], partner),
+    ]
+    for copy in halo + near:
+        copy.start()
     diagonal = eye(n)
     for load in loads[:2]:
         load.wait()
@@ -180,21 +188,6 @@
     v = coupling[1] * bonds[1:2, :].astype(jnp.float32)
     v = jnp.where(rank == 0, v, v.T)
     lead = jnp.where(rank == 0, product(w_near, w_near, ROWS), jnp.where(diagonal, LEAD_WIDTH, 0.0))
-    pl.semaphore_wait(barrier, len(peers))
-
-    def remote(source, target, send, recv, device):
-        return pltpu.make_async_remote_copy(source, target, send, recv, device_id=device, device_id_type=MESH)
-
-    halo = [
-        remote(own_in, before, halo_send.at[0], halo_recv.at[0], following),
-        remote(own_in, after, halo_send.at[1], halo_recv.at[1], previous),
-    ]
-    near = [
-        remote(coupling_in.at[0], near_w, near_send.at[0], near_recv.at[0], partner),
-        remote(bonds_in, near_b, near_send.at[1], near_recv.at[1], partner),
-    ]
-    for copy in halo + near:
-        copy.start()
     for load in loads[2:]:
         load.wait()
     for copy in halo:
@@ -282,6 +275,7 @@
             green[e, rank, 0] = outer_x[e, 0] + z[:n]
             green[e, rank, 1] = outer_x[e, 1] + z[n:]
 
+    sent = []
     buffers = [line_0, line_1, line_2]
     arrivals = [line_recv_0, line_recv_1, line_recv_2]
     for stage, a in enumerate((2, 1, 0)):
@@ -293,6 +287,7 @@
         ]
         for copy in copies:
             copy.start()
+        sent += copies
         buffer[mine] = partials[stage]
         if stage == 0:
             finish()
@@ -306,8 +301,19 @@
             partials[stage + 1] = total
         else:
             density[...] = (-2.0 * HALF_WINDOW / (devices * energies) / jnp.pi) * total
-        for copy in copies:
-            copy.wait_send()
+    for copy in sent:
+        copy.wait_send()
+
+
+def write(green, density, green_out, density_out, sem):
+    copies = [
+        pltpu.make_async_copy(density, density_out, sem.at[0]),
+        pltpu.make_async_copy(green, green_out, sem.at[1]),
+    ]
+    for copy in copies:
+        copy.start()
+    for copy in copies:
+        copy.wait()
 
 
 def shards(hamiltonian, coupling, bonds, phonon_coupling, previous_green, phonon_shift):
@@ -318,12 +324,13 @@
     square = pltpu.VMEM((energies, n, n), jnp.float32)
     halo = pltpu.VMEM(previous_green.shape, jnp.float32)
     dma = pltpu.SemaphoreType.DMA
-    return pl.pallas_call(
+    results = (
+        jax.ShapeDtypeStruct((energies, slabs, 2, n, n), jnp.float32),
+        jax.ShapeDtypeStruct((slabs, n), jnp.float32),
+    )
+    found = pl.pallas_call(
         sweep,
-        out_shape=(
-            jax.ShapeDtypeStruct((energies, slabs, 2, n, n), jnp.float32),
-            jax.ShapeDtypeStruct((slabs, n), jnp.float32),
-        ),
+        out_shape=results,
         in_specs=[HBM] * 6,
         out_specs=(VMEM, VMEM),
         scratch_shapes=[
@@ -341,6 +348,15 @@
         pltpu.with_memory_space_constraint(x, pltpu.HBM)
         for x in (hamiltonian, coupling, bonds, phonon_coupling, phonon_shift, previous_green)
     ])
+    return pl.pallas_call(
+        write,
+        out_shape=results,
+        in_specs=[VMEM] * 2,
+        out_specs=(HBM, HBM),
+        scratch_shapes=[dma((2,))],
+        compiler_params=pltpu.CompilerParams(vmem_limit_bytes=16 << 20),
+        name="write",
+    )(*found)
 
 
 def solution(mesh):

time: 51.3 us -> 50.4 us (0.982)
  local copies, waits for them, and re-layouts: 1.36 us -> 0 us
    unnamed x2 -> x0, local copies, waits for them, and re-layouts: 1.36 us -> none
    pallas_call x1 -> x2, Pallas kernels: 49.2 us -> 49.4 us  [the longest x1 48.6 us: shards(): pl.pallas_call(sweep, out_shape=results, in_specs=[HBM] * 6, out_specs=(V...]
where the time goes in v4:
time: 50.4 us; the launch traced here: 50.2 us
  Pallas kernels  49.4 us (98%)
  between operations  0.8 us (2%)
    pallas_call x1, Pallas kernels, shards(): pl.pallas_call(sweep, out_shape=results, in_specs=[HBM] * 6, out_specs=(V...  48.6 us

profile of v4, /device:TPU:8, one launch (start us, length us, event | category | flops | bytes accessed | tf_op | source)
XLA Modules:
  0.0 50.2 jit_solution(18394277929196118529)
XLA Ops:
  0.6 48.6 %sweep.1 = (f32[2,2,2,128,128]{4,3,2,1,0:T(8,128)S(1)}, f32[2,128]{1,0:T(2,128)S(1)}) custom-call(f32[2,128,128]{2,1,0:T(8,128)} %ham_in.1, f32[2,128,128]{2,1,0:T(8,128)} %coupling_in.1, s32[2,128]{1,0:T(2,128)} %bonds_in.1, f32[2,128]{1,0:T(2,128)} %strength_in.1, s32[2]{0:T(128)} %shifts_in.1, f32[2,2,2,128]{3,2,1,0:T(2,128)} %own_in.1), custom_call_target="tpu_custom_call" | custom-call | tf_op jit(solution)/shard_map/sweep/pallas_call | solution.py:331
  49.3 0.8 %write.1 = (f32[2,2,2,128,128]{4,3,2,1,0:T(8,128)}, f32[2,128]{1,0:T(2,128)}) custom-call(f32[2,2,2,128,128]{4,3,2,1,0:T(8,128)S(1)} %get-tuple-element.4.green, f32[2,128]{1,0:T(2,128)S(1)} %get-tuple-element.5.density), custom_call_target="tpu_custom_call" | custom-call | tf_op jit(solution)/shard_map/write/pallas_call | solution.py:351

commit v5 on v4

--- a/solution.py
+++ b/solution.py
@@ -133,8 +133,8 @@
 def sweep(
     ham_in, coupling_in, bonds_in, strength_in, shifts_in, own_in, green, density,
     ham, coupling, bonds, strength, shifts, own, before, after, near_w, near_b, outer_x, outer_u, inner_s, send_x, recv_x, real, imag,
-    partials, line_0, line_1, line_2, halo_send, halo_recv, near_send, near_recv, x_send, x_recv,
-    line_send, line_recv_0, line_recv_1, line_recv_2, load_sem,
+    partials, plane_parts, line_parts, halo_send, halo_recv, near_send, near_recv, x_send, x_recv,
+    part_send, plane_recv, line_recv, load_sem,
 ):
     loads = [
         pltpu.make_async_copy(source, target, load_sem.at[i])
@@ -157,12 +157,15 @@
 
     following, previous = along(1), along(devices - 1)
     partner = (*place, 1 - rank)
-    lines = [
-        [(*place[:a], lax.rem(place[a] + step, sizes[a]), *place[a + 1 :], rank) for step in range(1, sizes[a])]
-        for a in range(3)
-    ]
+    plane = [
+        (place[0], lax.rem(place[1] + y, sizes[1]), lax.rem(place[2] + x, sizes[2]), rank)
+        for y in range(sizes[1])
+        for x in range(sizes[2])
+        if y or x
+    ]
+    line = [(lax.rem(place[0] + step, sizes[0]), place[1], place[2], rank) for step in range(1, sizes[0])]
     barrier = pltpu.get_barrier_semaphore()
-    peers = [following, previous, partner] + lines[0] + lines[1] + lines[2]
+    peers = [following, previous, partner] + plane + line
     for peer in peers:
         pl.semaphore_signal(barrier, inc=1, device_id=peer, device_id_type=MESH)
 
@@ -276,29 +279,33 @@
             green[e, rank, 1] = outer_x[e, 1] + z[n:]
 
     sent = []
-    buffers = [line_0, line_1, line_2]
-    arrivals = [line_recv_0, line_recv_1, line_recv_2]
-    for stage, a in enumerate((2, 1, 0)):
-        buffer, arrival, mine = buffers[a], arrivals[a], place[a]
-        source = partials.at[stage]
+
+    def in_plane(device):
+        return device[1] * sizes[2] + device[2]
+
+    def in_line(device):
+        return device[0]
+
+    for stage, (group, slot, parts, arrival) in enumerate(
+        ((plane, in_plane, plane_parts, plane_recv), (line, in_line, line_parts, line_recv))
+    ):
+        source, mine = partials.at[stage], slot((*place, rank))
         copies = [
-            remote(source, buffer.at[mine], line_send.at[a, step], arrival.at[mine], device)
-            for step, device in enumerate(lines[a])
+            remote(source, parts.at[mine], part_send.at[stage, i], arrival.at[mine], device)
+            for i, device in enumerate(group)
         ]
         for copy in copies:
             copy.start()
         sent += copies
-        buffer[mine] = partials[stage]
+        parts[mine] = partials[stage]
         if stage == 0:
             finish()
-        for step in range(1, sizes[a]):
-            sender = lax.rem(mine + step, sizes[a])
-            remote(source, buffer.at[sender], line_send.at[a, step - 1], arrival.at[sender], lines[a][step - 1]).wait_recv()
-        total = buffer[0]
-        for other in range(1, sizes[a]):
-            total = total + buffer[other]
-        if stage < 2:
-            partials[stage + 1] = total
+        for i, device in enumerate(group):
+            sender = slot(device)
+            remote(source, parts.at[sender], part_send.at[stage, i], arrival.at[sender], device).wait_recv()
+        total = total_of([parts[i] for i in range(len(group) + 1)])
+        if stage == 0:
+            partials[1] = total
         else:
             density[...] = (-2.0 * HALF_WINDOW / (devices * energies) / jnp.pi) * total
     for copy in sent:
@@ -319,7 +326,7 @@
 def shards(hamiltonian, coupling, bonds, phonon_coupling, previous_green, phonon_shift):
     energies, slabs, n = previous_green.shape[0], hamiltonian.shape[0], hamiltonian.shape[1]
     sizes = [lax.axis_size(axis) for axis in ENERGY]
-    longest = max(sizes)
+    places = (sizes[1] * sizes[2], sizes[0])
     block = pltpu.VMEM((energies, 2, n, n), jnp.float32)
     square = pltpu.VMEM((energies, n, n), jnp.float32)
     halo = pltpu.VMEM(previous_green.shape, jnp.float32)
@@ -337,10 +344,10 @@
             *[pltpu.VMEM(x.shape, x.dtype) for x in (hamiltonian, coupling, bonds, phonon_coupling)],
             pltpu.SMEM(phonon_shift.shape, jnp.int32), halo, halo, halo, pltpu.VMEM((n, n), jnp.float32), pltpu.VMEM(bonds.shape, jnp.int32),
             block, block, block, block, block, square, square,
-            pltpu.VMEM((3, slabs, n), jnp.float32),
-            *[pltpu.VMEM((size, slabs, n), jnp.float32) for size in sizes],
+            pltpu.VMEM((2, slabs, n), jnp.float32),
+            *[pltpu.VMEM((size, slabs, n), jnp.float32) for size in places],
             dma((2,)), dma((2,)), dma((2,)), dma((2,)), dma((1,)), dma((1,)),
-            dma((3, longest)), *[dma((size,)) for size in sizes], dma((6,)),
+            dma((2, max(places))), *[dma((size,)) for size in places], dma((6,)),
         ],
         compiler_params=pltpu.CompilerParams(collective_id=0, has_side_effects=True, vmem_limit_bytes=16 << 20),
         name="sweep",

time: 50.4 us -> 50.5 us (level)
  no operation moved by 1% of the time
where the time goes in v5:
time: 50.5 us; the launch traced here: 50.4 us
  Pallas kernels  49.6 us (98%)
  between operations  0.8 us (2%)
    pallas_call x1, Pallas kernels, shards(): pl.pallas_call(sweep, out_shape=results, in_specs=[HBM] * 6, out_specs=(V...  48.8 us

profile of v5, /device:TPU:8, one launch (start us, length us, event | category | flops | bytes accessed | tf_op | source)
XLA Modules:
  0.0 50.4 jit_solution(9885599744966024601)
XLA Ops:
  0.6 48.8 %sweep.1 = (f32[2,2,2,128,128]{4,3,2,1,0:T(8,128)S(1)}, f32[2,128]{1,0:T(2,128)S(1)}) custom-call(f32[2,128,128]{2,1,0:T(8,128)} %ham_in.1, f32[2,128,128]{2,1,0:T(8,128)} %coupling_in.1, s32[2,128]{1,0:T(2,128)} %bonds_in.1, f32[2,128]{1,0:T(2,128)} %strength_in.1, s32[2]{0:T(128)} %shifts_in.1, f32[2,2,2,128]{3,2,1,0:T(2,128)} %own_in.1), custom_call_target="tpu_custom_call" | custom-call | tf_op jit(solution)/shard_map/sweep/pallas_call | solution.py:338
  49.4 0.8 %write.1 = (f32[2,2,2,128,128]{4,3,2,1,0:T(8,128)}, f32[2,128]{1,0:T(2,128)}) custom-call(f32[2,2,2,128,128]{4,3,2,1,0:T(8,128)S(1)} %get-tuple-element.4.green, f32[2,128]{1,0:T(2,128)S(1)} %get-tuple-element.5.density), custom_call_target="tpu_custom_call" | custom-call | tf_op jit(solution)/shard_map/write/pallas_call | solution.py:358
